TPU v7x, 512 devices: a whole 4x8x8 slice. The times are simulated.
512 devices in a mesh: dp: 32 (over y_hi, z), inblk: 4 (over x), outcol: 4 (over y_lo, core).
Axes of the slice: x: 4, y: 8 (y_hi: 4, y_lo: 2; y = y_hi * 2 + y_lo), z: 8, core: 2. Of those that a mesh axis runs over, the one named last changes fastest.
Arguments:
- activations: bfloat16 [4096, 8192], P('dp', ('inblk', 'outcol')), may hold values from -1.5 to 1.5
- cotangent: bfloat16 [4096, 1024], P('dp', 'outcol'), may hold values from -6 to 6
- base_weight: bfloat16 [8192, 1024], P('inblk', 'outcol'), may hold values from -0.09375 to 0.09375
- skew_param: float32 [32, 256, 256], P(('inblk', 'outcol'), 'dp'), may hold values from -0.3125 to 0.3125
Outputs:
- grad_acts: bfloat16 [4096, 8192], P('dp', ('inblk', 'outcol'))
- grad_skew: float32 [32, 256, 256], P(('inblk', 'outcol'), 'dp')
All inputs are finite; a program needn't handle non-finite values.
Results may differ from a plain program's by a relative error of at most 0.0058.
Values may be sent and summed in bfloat16 or wider, within the bound.
No kernel may reach another device: no remote copies, remote signals or barrier semaphores. Data moves between devices by JAX's collectives and lax.ppermute only.
A program may use at most 64 MiB of HBM per device.

v0:
```python
import jax
import jax.numpy as jnp
from jax import lax
from jax.sharding import PartitionSpec as P


def high_product(left, right):
    return jnp.matmul(left, right, precision=lax.Precision.HIGHEST)


def power_list(skew_input):
    skew_mat = skew_input - jnp.swapaxes(skew_input, -1, -2)
    powers = [skew_mat]
    for degree in range(5):
        powers.append(high_product(powers[-1], skew_mat))
    return powers


def rotation_of(powers):
    block_width = powers[0].shape[-1]
    identity_mat = jnp.eye(block_width, dtype=jnp.float32)
    series = powers[0] + powers[1] + powers[2] + powers[3] + powers[4]
    return identity_mat + 2.0 * series + powers[5]


def chain_rule(grad_rot, powers):
    negated = [powers[degree] * (-1.0) ** (degree + 1) for degree in range(5)]
    partial_value = grad_rot
    running = 2.0 * grad_rot
    for degree in range(2, 7):
        partial_value = high_product(negated[0], partial_value) + high_product(
            grad_rot, negated[degree - 2]
        )
        weight_factor = 2.0 if degree < 6 else 1.0
        running = running + weight_factor * partial_value
    return running - jnp.swapaxes(running, -1, -2)


def body(activations, cotangent, base_weight, skew_param):
    full_skew = lax.all_gather(skew_param, "dp", axis=1, tiled=True)
    powers = power_list(full_skew)
    rotation = rotation_of(powers).astype(jnp.bfloat16)
    token_count = activations.shape[0]
    own_width = activations.shape[1]
    block_count = full_skew.shape[0]
    block_width = full_skew.shape[2]
    features = lax.psum_scatter(
        lax.dot_general(
            base_weight, cotangent, (((1,), (1,)), ((), ())), preferred_element_type=jnp.float32
        ),
        "outcol",
        scatter_dimension=0,
        tiled=True,
    )
    features = features.astype(jnp.bfloat16).reshape(block_count, block_width, token_count)
    grad_t = jnp.einsum(
        "bij,bjt->bit", rotation, features, preferred_element_type=jnp.float32
    ).astype(jnp.bfloat16)
    grad_acts = jnp.transpose(grad_t.reshape(own_width, token_count))
    grad_rot = jnp.einsum(
        "tbi,bjt->bij",
        activations.reshape(token_count, block_count, block_width),
        features,
        preferred_element_type=jnp.float32,
    )
    summed = lax.psum(grad_rot, "dp")
    grad_full = chain_rule(summed, powers)
    share_rows = block_width // lax.axis_size("dp")
    grad_skew = lax.dynamic_slice_in_dim(
        grad_full, lax.axis_index("dp") * share_rows, share_rows, 1
    )
    return (grad_acts, grad_skew)


def solution(mesh):
    return jax.shard_map(
        body,
        mesh=mesh,
        in_specs=(
            P("dp", ("inblk", "outcol")),
            P("dp", "outcol"),
            P("inblk", "outcol"),
            P(("inblk", "outcol"), "dp", None),
        ),
        out_specs=(P("dp", ("inblk", "outcol")), P(("inblk", "outcol"), "dp", None)),
        check_vma=False,
    )
```

profile of v0, /device:TPU:6, one launch (start us, length us, event | category | flops | bytes accessed | tf_op | source)
XLA Modules:
  0.0 434.6 jit_solution(13331793487568071938)
XLA Ops:
  7.2 0.0 copy-start
  7.2 0.0 reduce-scatter.2.cloned.1.call-start
  7.2 1.2 copy-done
  8.4 2.2 fusion.38
  10.6 0.0 copy-start.4
  10.6 0.0 reduce-scatter.2.cloned.1.call-update
  10.7 0.0 all-reduce.2.cloned.1.call-start
  10.7 0.6 copy-done.4
  11.4 92.0 %all_gather.3 = f32[2,256,256]{2,0,1:T(2,128)S(1)} all-gather(f32[2,8,256]{2,0,1:T(2,128)S(1)} %copy.12), channel_id=1, replica_groups=mesh['dp'=32,'inblk'=4,'outcol'=4] {'dp'}, dimensions={1}, use_global_device_ids=true | all-gather | bytes 540672 | tf_op jit(solution)/shard_map/all_gather | solution.py:40
  103.4 0.2 copy.13
  103.7 0.1 bitcast_subtract_fusion
  103.7 0.6 fusion.34
  104.4 0.7 fusion.35
  105.0 0.7 fusion.36
  105.7 1.5 fusion.37
  107.2 0.0 reduce-scatter.2.cloned.1.call-done
  107.2 0.0 copy-start.3
  107.2 1.0 convert_element_type.18
  108.2 0.0 copy-done.3
  108.2 1.1 convolution_bitcast_fusion
  109.3 0.0 all-reduce.2.cloned.1.call-update
  109.3 1.9 fusion.1
  111.2 0.2 convolution_convert_fusion
  111.4 0.8 copy.15
  112.2 306.5 %all-reduce.2.cloned.1.call-done = f32[2,256,256]{2,1,0:T(8,128)} async-done(((f32[2,256,256]{2,1,0:T(8,128)}), f32[2,256,256]{2,1,0:T(8,128)}) %all-reduce.2.cloned.1.call-update) | async-done | bytes 524304 | tf_op jit(solution)/shard_map/psum | solution.py:66
  418.7 0.0 copy-start.1
  418.7 1.8 fusion.13
  420.5 0.0 copy-done.1
  420.5 0.7 convolution_add_fusion.4
  421.2 0.7 fusion.10
  421.8 0.7 convolution_add_fusion.3
  422.5 0.7 fusion.8
  423.2 0.7 convolution_add_fusion.2
  423.9 0.7 fusion.6
  424.5 0.7 convolution_add_fusion.1
  425.2 0.0 copy-start.2
  425.2 0.7 fusion.4
  425.9 0.4 copy-done.2
  426.2 0.7 fusion
  427.0 0.2 copy.18
  427.2 0.6 dynamic-slice_subtract_fusion
  (2 shorter events, 0.0 us)
Async XLA Ops:
  7.2 1.2 copy-start
  7.2 100.0 %reduce-scatter.2.cloned.1.call-start = ((), (), s32[]{:S(2)}) async-start(), calls=%async_computation.1 | async-start | bytes 1310720 | tf_op jit(solution)/shard_map/reduce_scatter | solution.py:47
  10.6 0.7 copy-start.4
  10.7 408.0 %all-reduce.2.cloned.1.call-start = ((), (), s32[]{:S(2)}) async-start(), calls=%async_computation.2 | async-start | bytes 1048576 | tf_op jit(solution)/shard_map/psum | solution.py:66
  107.2 1.0 copy-start.3
  418.7 1.8 copy-start.1
  425.2 1.0 copy-start.2
Sparse Core Ops, SparseCore 0:
  10.9 31.1 reduce-scatter.1
  109.4 309.2 all-reduce.1
where the time goes:
time: 435 us
  waiting for transfers between devices  307 us (71%)
  blocking collectives  92 us (21%)
  matrix products  16.7 us (4%)
  between operations  14.2 us (3%)
    psum x1, waiting for transfers between devices, body(): summed = lax.psum(grad_rot, 'dp')  306 us
    all_gather x1, blocking collectives, body(): full_skew = lax.all_gather(skew_param, 'dp', axis=1, tiled=True)  92 us
    dot_general x15, matrix products, high_product(): return jnp.matmul(left, right, precision=lax.Precision.HIGHEST)  13.2 us
  transfers between devices with their start and end apart: 2, of which 1 were waited for; matrix products, arithmetic and copies ran while one was open for 2% of the time, Pallas kernels for 0%

commit v1 on v0

v1 whole, which is shorter than its diff:
```python
import jax
import jax.numpy as jnp
from jax import lax
from jax.experimental import pallas as pl
from jax.experimental.pallas import tpu as pltpu
from jax.sharding import PartitionSpec as P

BF16 = jnp.bfloat16
F32 = jnp.float32


def split(x):
    high = x.astype(BF16)
    return high, (x - high.astype(F32)).astype(BF16)


def product(left, right):
    dot = lambda a, b: jnp.dot(a, b, preferred_element_type=F32)
    return dot(left[0], right[0]) + (dot(left[0], right[1]) + dot(left[1], right[0]))


def factors(gathered, block):
    width = gathered.shape[-1]
    param = gathered[:, block].reshape(width, width)
    skew = param - param.T
    skew_pair = split(skew)
    square = product(skew_pair, skew_pair)
    square_pair = split(square)
    fourth = product(square_pair, square_pair)
    return skew, skew_pair, square, square_pair, square + fourth


def features_kernel(cotangent_ref, weight_ref, out_ref):
    out_ref[0] = lax.dot_general(
        cotangent_ref[...], weight_ref[...], (((1,), (1,)), ((), ())), preferred_element_type=F32
    ).astype(BF16)


def block_grad_kernel(parts_ref, acts_ref, features_ref, grad_ref):
    blocks, width = grad_ref.shape[0], grad_ref.shape[-1]
    total = parts_ref[0].astype(F32)
    for part in range(1, parts_ref.shape[0]):
        total = total + parts_ref[part].astype(F32)
    features = total.astype(BF16)
    features_ref[...] = features
    acts = acts_ref[...]
    for block in range(blocks):
        cols = slice(block * width, (block + 1) * width)
        grad_ref[block] = lax.dot_general(
            acts[:, cols], features[:, cols], (((0,), (0,)), ((), ())), preferred_element_type=F32
        )


def chain_kernel(gathered_ref, grad_ref, out_ref):
    shares, blocks, rows, width = gathered_ref.shape
    pieces = []
    for block in range(blocks):
        skew, skew_pair, square, square_pair, rest = factors(gathered_ref, block)
        grad = grad_ref[block]
        grad_pair = split(grad)
        left_bar = grad + product(grad_pair, split(rest))
        right_bar = grad + product(split(square - 2.0 * skew), grad_pair)
        right_sym = right_bar + right_bar.T
        both = left_bar + product(split(right_sym), square_pair)
        square_sym = right_sym + both + both.T
        total = 2.0 * left_bar - product(split(square_sym), skew_pair)
        pieces.append((total - total.T).reshape(shares, rows, width))
    out_ref[...] = jnp.concatenate(pieces, axis=1).astype(BF16)


def acts_kernel(gathered_ref, features_ref, out_ref):
    blocks, width = gathered_ref.shape[1], gathered_ref.shape[-1]
    for block in range(blocks):
        skew, _, square, _, rest = factors(gathered_ref, block)
        first = 2.0 * skew + square
        row = lax.broadcasted_iota(jnp.int32, (width, width), 0)
        col = lax.broadcasted_iota(jnp.int32, (width, width), 1)
        identity = jnp.where(row == col, 1.0, 0.0).astype(F32)
        rotation = (identity + first + rest + product(split(first), split(rest))).astype(BF16)
        cols = slice(block * width, (block + 1) * width)
        out_ref[:, cols] = lax.dot_general(
            features_ref[:, cols], rotation, (((1,), (1,)), ((), ())), preferred_element_type=F32
        ).astype(BF16)


def sum_kernel(parts_ref, out_ref):
    out_ref[...] = jnp.sum(parts_ref[...].astype(F32), axis=0)


def body(activations, cotangent, base_weight, skew_param):
    shares = lax.axis_size("dp")
    parts = lax.axis_size("outcol")
    tokens, own_width = activations.shape
    depth = cotangent.shape[1]
    blocks, rows, width = skew_param.shape
    gathered = lax.all_to_all(
        jnp.broadcast_to(skew_param[None], (shares, blocks, rows, width)), "dp", 0, 0, tiled=True
    )
    partial = pl.pallas_call(
        features_kernel,
        grid=(parts,),
        in_specs=[
            pl.BlockSpec((tokens, depth), lambda i: (0, 0)),
            pl.BlockSpec((own_width, depth), lambda i: (i, 0)),
        ],
        out_specs=pl.BlockSpec((1, tokens, own_width), lambda i: (i, 0, 0)),
        out_shape=jax.ShapeDtypeStruct((parts, tokens, own_width), BF16),
        cost_estimate=pl.CostEstimate(
            flops=2 * tokens * depth * own_width * parts, bytes_accessed=1 << 21, transcendentals=0
        ),
    )(cotangent, base_weight)
    received = lax.all_to_all(partial, "outcol", 0, 0, tiled=True)
    features, grad_rot = pl.pallas_call(
        block_grad_kernel,
        out_shape=(
            jax.ShapeDtypeStruct((tokens, own_width), BF16),
            jax.ShapeDtypeStruct((blocks, width, width), F32),
        ),
        cost_estimate=pl.CostEstimate(
            flops=2 * tokens * own_width * width, bytes_accessed=1 << 21, transcendentals=0
        ),
    )(received, activations)
    sends = pl.pallas_call(
        chain_kernel,
        out_shape=jax.ShapeDtypeStruct((shares, blocks * rows, width), BF16),
        cost_estimate=pl.CostEstimate(
            flops=2 * 18 * blocks * width**3, bytes_accessed=3 << 20, transcendentals=0
        ),
    )(gathered, grad_rot)
    arrived = lax.all_to_all(sends, "dp", 0, 0, tiled=True)
    grad_acts = pl.pallas_call(
        acts_kernel,
        out_shape=jax.ShapeDtypeStruct((tokens, own_width), BF16),
        cost_estimate=pl.CostEstimate(
            flops=2 * 10 * blocks * width**3, bytes_accessed=1 << 20, transcendentals=0
        ),
    )(gathered, features)
    grad_skew = pl.pallas_call(
        sum_kernel,
        out_shape=jax.ShapeDtypeStruct((blocks * rows, width), F32),
    )(arrived).reshape(blocks, rows, width)
    return grad_acts, grad_skew


def solution(mesh):
    return jax.shard_map(
        body,
        mesh=mesh,
        in_specs=(
            P("dp", ("inblk", "outcol")),
            P("dp", "outcol"),
            P("inblk", "outcol"),
            P(("inblk", "outcol"), "dp", None),
        ),
        out_specs=(P("dp", ("inblk", "outcol")), P(("inblk", "outcol"), "dp", None)),
        check_vma=False,
    )
```

time: 435 us -> 81.7 us (0.19)
  waiting for transfers between devices: 307 us -> 26.5 us
  blocking collectives: 92 us -> 13.2 us
  starting transfers between devices: 0.08 us -> 22.3 us
  matrix products: 16.7 us -> 0 us
  Pallas kernels: 0 us -> 16.2 us
  between operations: 14.2 us -> 0.65 us
    psum x1 -> x0, waiting for transfers between devices: 306 us -> none  [body(): summed = lax.psum(grad_rot, 'dp')]
    all_gather x1 -> x0, blocking collectives: 92 us -> none  [body(): full_skew = lax.all_gather(skew_param, 'dp', axis=1, tiled=True)]
    all_to_all x0 -> x2, waiting for transfers between devices: none -> 26.5 us  [the longest x1 16.3 us: body(): lax.all_to_all(jnp.broadcast_to(skew_param[None], (shares, blocks, rows,...]
    all_to_all x0 -> x2, starting transfers between devices: none -> 22.3 us  [the longest x1 16 us: body(): lax.all_to_all(jnp.broadcast_to(skew_param[None], (shares, blocks, rows,...]
    dot_general x18 -> x0, matrix products: 16.7 us -> none  [the longest x15 13.2 us: high_product(): return jnp.matmul(left, right, precision=lax.Precision.HIGHEST)]
    pallas_call x0 -> x5, Pallas kernels: none -> 16.2 us  [the longest x1 4.82 us: body(): pl.pallas_call(chain_kernel, out_shape=jax.ShapeDtypeStruct((shares, bloc...]
    all_to_all x0 -> x1, blocking collectives: none -> 13.2 us  [body(): received = lax.all_to_all(partial, 'outcol', 0, 0, tiled=True)]
  transfers between devices with their start and end apart: 2 -> 2, of which waited for: 1 -> 2; matrix products, arithmetic and copies ran while one was open for 2% -> 0% of each run, Pallas kernels for 0% -> 8%
where the time goes in v1:
time: 81.7 us; the launch traced here: 81.2 us
  waiting for transfers between devices  26.5 us (32%)
  starting transfers between devices  22.3 us (27%)
  Pallas kernels  16.2 us (20%)
  blocking collectives  13.2 us (16%)
  local copies, waits for them, and re-layouts  2.36 us (3%)
    all_to_all x1, waiting for transfers between devices, body(): lax.all_to_all(jnp.broadcast_to(skew_param[None], (shares, blocks, rows,...  16.3 us
    all_to_all x1, starting transfers between devices, body(): lax.all_to_all(jnp.broadcast_to(skew_param[None], (shares, blocks, rows,...  16 us
    all_to_all x1, blocking collectives, body(): received = lax.all_to_all(partial, 'outcol', 0, 0, tiled=True)  13.2 us
    all_to_all x1, waiting for transfers between devices, body(): arrived = lax.all_to_all(sends, 'dp', 0, 0, tiled=True)  10.2 us
    all_to_all x1, starting transfers between devices, body(): arrived = lax.all_to_all(sends, 'dp', 0, 0, tiled=True)  6.37 us
    pallas_call x1, Pallas kernels, body(): pl.pallas_call(chain_kernel, out_shape=jax.ShapeDtypeStruct((shares, bloc...  4.82 us
    pallas_call x1, Pallas kernels, body(): pl.pallas_call(acts_kernel, out_shape=jax.ShapeDtypeStruct((tokens, own_w...  3.97 us
    pallas_call x1, Pallas kernels, body(): pl.pallas_call(features_kernel, grid=(parts,), in_specs=[pl.BlockSpec((to...  3.68 us
  transfers between devices with their start and end apart: 2, of which 2 were waited for; matrix products, arithmetic and copies ran while one was open for 0% of the time, Pallas kernels for 8%

profile of v1, /device:TPU:6, one launch (start us, length us, event | category | flops | bytes accessed | tf_op | source)
XLA Modules:
  0.0 81.2 jit_solution(13834161322897312621)
XLA Ops:
  0.6 3.7 %shard_map.59 = bf16[4,128,512]{2,1,0:T(8,128)(2,1)} custom-call(bf16[128,256]{1,0:T(8,128)(2,1)} %cotangent_ref.1, bf16[2048,256]{1,0:T(8,128)(2,1)} %weight_ref.1), custom_call_target="tpu_custom_call" | custom-call | flops 134217728 | bytes 2097152 | tf_op jit(solution)/shard_map/pallas_call | solution.py:99
  4.3 0.0 copy-start.2
  4.3 13.2 %all_to_all.15.parts_ref = bf16[4,128,512]{2,1,0:T(8,128)(2,1)} all-to-all(bf16[4,128,512]{2,1,0:T(8,128)(2,1)} %shard_map.59), channel_id=1, replica_groups=mesh['dp'=32,'inblk'=4,'outcol'=4] {'outcol'}, dimensions={0} | all-to-all | bytes 1048576 | tf_op jit(solution)/shard_map/all_to_all | solution.py:112
  17.5 0.0 copy-done.2
  17.5 0.9 %broadcast_in_dim.2 = f32[32,2,8,256]{3,2,1,0:T(8,128)} broadcast(f32[2,8,256]{2,1,0:T(8,128)S(1)} %copy-done.2), dimensions={1,2,3} | broadcast | bytes 540672 | tf_op jit(solution)/shard_map/broadcast_in_dim | solution.py:97
  18.4 16.0 %all-to-all-start = ((f32[32,2,8,256]{3,2,1,0:T(8,128)}), f32[32,2,8,256]{3,2,1,0:T(8,128)S(1)}, u32[]{:S(2)}, u32[]{:S(2)}) async-start(f32[32,2,8,256]{3,2,1,0:T(8,128)} %broadcast_in_dim.2), calls=%async_computation | async-start | bytes 1048576 | tf_op jit(solution)/shard_map/all_to_all | solution.py:96
  34.3 2.1 %shard_map.60 = (bf16[128,512]{1,0:T(8,128)(2,1)}, f32[2,256,256]{2,1,0:T(8,128)}) custom-call(bf16[4,128,512]{2,1,0:T(8,128)(2,1)} %all_to_all.15.parts_ref, bf16[128,512]{1,0:T(8,128)(2,1)} %acts_ref.1), custom_call_target="tpu_custom_call" | custom-call | flops 33554432 | bytes 2097152 | tf_op jit(solution)/shard_map/pallas_call | solution.py:113
  36.5 16.3 %all-to-all-done.gathered_ref = f32[32,2,8,256]{3,2,1,0:T(8,128)S(1)} async-done(((f32[32,2,8,256]{3,2,1,0:T(8,128)}), f32[32,2,8,256]{3,2,1,0:T(8,128)S(1)}, u32[]{:S(2)}, u32[]{:S(2)}) %all-to-all-start) | async-done | bytes 524320 | tf_op jit(solution)/shard_map/all_to_all | solution.py:96
  52.8 0.0 copy-start.1
  52.8 0.8 copy-done.1
  53.6 4.8 %shard_map.62 = bf16[32,16,256]{2,1,0:T(8,128)(2,1)} custom-call(f32[32,2,8,256]{3,2,1,0:T(8,128)} %copy-done.1, f32[2,256,256]{2,1,0:T(8,128)} %get-tuple-element.5.grad_ref), custom_call_target="tpu_custom_call" | custom-call | flops 1207959552 | bytes 3145728 | tf_op jit(solution)/shard_map/pallas_call | solution.py:123
  58.4 6.4 %all-to-all-start.2 = ((bf16[32,16,256]{2,1,0:T(8,128)(2,1)}), bf16[32,16,256]{2,1,0:T(8,128)(2,1)S(1)}, u32[]{:S(2)}, u32[]{:S(2)}) async-start(bf16[32,16,256]{2,1,0:T(8,128)(2,1)} %shard_map.62), calls=%async_computation.2 | async-start | bytes 524288 | tf_op jit(solution)/shard_map/all_to_all | solution.py:130
  64.8 4.0 %shard_map.61 = bf16[128,512]{1,0:T(8,128)(2,1)} custom-call(f32[32,2,8,256]{3,2,1,0:T(8,128)} %copy-done.1, bf16[128,512]{1,0:T(8,128)(2,1)} %get-tuple-element.4.features_ref), custom_call_target="tpu_custom_call" | custom-call | flops 671088640 | bytes 1048576 | tf_op jit(solution)/shard_map/pallas_call | solution.py:131
  68.7 10.2 %all-to-all-done.2.parts_ref = bf16[32,16,256]{2,1,0:T(8,128)(2,1)S(1)} async-done(((bf16[32,16,256]{2,1,0:T(8,128)(2,1)}), bf16[32,16,256]{2,1,0:T(8,128)(2,1)S(1)}, u32[]{:S(2)}, u32[]{:S(2)}) %all-to-all-start.2) | async-done | bytes 262176 | tf_op jit(solution)/shard_map/all_to_all | solution.py:130
  78.9 0.0 copy-start
  78.9 0.7 copy-done
  79.6 1.6 %shard_map.63 = f32[16,256]{1,0:T(8,128)} custom-call(bf16[32,16,256]{2,1,0:T(8,128)(2,1)} %copy-done), custom_call_target="tpu_custom_call" | custom-call | tf_op jit(solution)/shard_map/pallas_call | solution.py:138
Async XLA Ops:
  4.3 13.2 %copy-start.2 = (f32[2,8,256]{2,1,0:T(8,128)S(1)}, f32[2,8,256]{2,1,0:T(8,128)}, u32[]{:S(2)}) copy-start(f32[2,8,256]{2,1,0:T(8,128)} %param.7) | copy-start | bytes 49156
  18.4 34.4 %all-to-all-start = ((f32[32,2,8,256]{3,2,1,0:T(8,128)}), f32[32,2,8,256]{3,2,1,0:T(8,128)S(1)}, u32[]{:S(2)}, u32[]{:S(2)}) async-start(f32[32,2,8,256]{3,2,1,0:T(8,128)} %broadcast_in_dim.2), calls=%async_computation | async-start | bytes 1048576 | tf_op jit(solution)/shard_map/all_to_all | solution.py:96
  52.8 0.8 copy-start.1
  58.4 20.5 %all-to-all-start.2 = ((bf16[32,16,256]{2,1,0:T(8,128)(2,1)}), bf16[32,16,256]{2,1,0:T(8,128)(2,1)S(1)}, u32[]{:S(2)}, u32[]{:S(2)}) async-start(bf16[32,16,256]{2,1,0:T(8,128)(2,1)} %shard_map.62), calls=%async_computation.2 | async-start | bytes 524288 | tf_op jit(solution)/shard_map/all_to_all | solution.py:130
  78.9 0.7 copy-start

commit v2 on v1

--- a/solution.py
+++ b/solution.py
@@ -30,17 +30,29 @@
     return skew, skew_pair, square, square_pair, square + fourth
 
 
-def features_kernel(cotangent_ref, weight_ref, out_ref):
-    out_ref[0] = lax.dot_general(
-        cotangent_ref[...], weight_ref[...], (((1,), (1,)), ((), ())), preferred_element_type=F32
-    ).astype(BF16)
+def features_kernel(cotangent_ref, weight_ref, own_ref, *sent_refs):
+    width = own_ref.shape[1]
+    me = lax.axis_index("outcol")
+    for turn in range(1 + len(sent_refs)):
+        first = pl.multiple_of((me ^ turn) * width, width)
+        part = lax.dot_general(
+            cotangent_ref[...],
+            weight_ref[pl.ds(first, width), :],
+            (((1,), (1,)), ((), ())),
+            preferred_element_type=F32,
+        )
+        if turn:
+            sent_refs[turn - 1][...] = part.astype(BF16)
+        else:
+            own_ref[...] = part
 
 
-def block_grad_kernel(parts_ref, acts_ref, features_ref, grad_ref):
+def block_grad_kernel(acts_ref, own_ref, *refs):
+    part_refs, (features_ref, grad_ref) = refs[:-2], refs[-2:]
     blocks, width = grad_ref.shape[0], grad_ref.shape[-1]
-    total = parts_ref[0].astype(F32)
-    for part in range(1, parts_ref.shape[0]):
-        total = total + parts_ref[part].astype(F32)
+    total = own_ref[...]
+    for part_ref in part_refs:
+        total = total + part_ref[...].astype(F32)
     features = total.astype(BF16)
     features_ref[...] = features
     acts = acts_ref[...]
@@ -83,8 +95,13 @@
         ).astype(BF16)
 
 
-def sum_kernel(parts_ref, out_ref):
-    out_ref[...] = jnp.sum(parts_ref[...].astype(F32), axis=0)
+def kernel_call(kernel, out_shape, flops, moved):
+    return pl.pallas_call(
+        kernel,
+        out_shape=out_shape,
+        compiler_params=pltpu.CompilerParams(vmem_limit_bytes=24 << 20),
+        cost_estimate=pl.CostEstimate(flops=flops, bytes_accessed=moved, transcendentals=0),
+    )
 
 
 def body(activations, cotangent, base_weight, skew_param):
@@ -93,52 +110,50 @@
     tokens, own_width = activations.shape
     depth = cotangent.shape[1]
     blocks, rows, width = skew_param.shape
+    scale = 65536.0
+    packed = (skew_param * scale).astype(jnp.float16)
     gathered = lax.all_to_all(
-        jnp.broadcast_to(skew_param[None], (shares, blocks, rows, width)), "dp", 0, 0, tiled=True
+        jnp.broadcast_to(packed.reshape(1, blocks * rows, width), (shares, blocks * rows, width)),
+        "dp",
+        0,
+        0,
+        tiled=True,
     )
-    partial = pl.pallas_call(
+    gathered = (gathered.astype(F32) * (1.0 / scale)).reshape(shares, blocks, rows, width)
+    own, *sent = kernel_call(
         features_kernel,
-        grid=(parts,),
-        in_specs=[
-            pl.BlockSpec((tokens, depth), lambda i: (0, 0)),
-            pl.BlockSpec((own_width, depth), lambda i: (i, 0)),
-        ],
-        out_specs=pl.BlockSpec((1, tokens, own_width), lambda i: (i, 0, 0)),
-        out_shape=jax.ShapeDtypeStruct((parts, tokens, own_width), BF16),
-        cost_estimate=pl.CostEstimate(
-            flops=2 * tokens * depth * own_width * parts, bytes_accessed=1 << 21, transcendentals=0
-        ),
+        [jax.ShapeDtypeStruct((tokens, own_width), F32)]
+        + [jax.ShapeDtypeStruct((tokens, own_width), BF16)] * (parts - 1),
+        2 * tokens * depth * own_width * parts,
+        2 << 20,
     )(cotangent, base_weight)
-    received = lax.all_to_all(partial, "outcol", 0, 0, tiled=True)
-    features, grad_rot = pl.pallas_call(
+    received = [
+        lax.ppermute(part, "outcol", [(i, i ^ turn) for i in range(parts)])
+        for turn, part in enumerate(sent, 1)
+    ]
+    features, grad_rot = kernel_call(
         block_grad_kernel,
-        out_shape=(
+        (
             jax.ShapeDtypeStruct((tokens, own_width), BF16),
             jax.ShapeDtypeStruct((blocks, width, width), F32),
         ),
-        cost_estimate=pl.CostEstimate(
-            flops=2 * tokens * own_width * width, bytes_accessed=1 << 21, transcendentals=0
-        ),
-    )(received, activations)
-    sends = pl.pallas_call(
+        2 * tokens * own_width * width,
+        2 << 20,
+    )(activations, own, *received)
+    sends = kernel_call(
         chain_kernel,
-        out_shape=jax.ShapeDtypeStruct((shares, blocks * rows, width), BF16),
-        cost_estimate=pl.CostEstimate(
-            flops=2 * 18 * blocks * width**3, bytes_accessed=3 << 20, transcendentals=0
-        ),
+        jax.ShapeDtypeStruct((shares, blocks * rows, width), BF16),
+        2 * 18 * blocks * width**3,
+        2 << 20,
     )(gathered, grad_rot)
     arrived = lax.all_to_all(sends, "dp", 0, 0, tiled=True)
-    grad_acts = pl.pallas_call(
+    grad_acts = kernel_call(
         acts_kernel,
-        out_shape=jax.ShapeDtypeStruct((tokens, own_width), BF16),
-        cost_estimate=pl.CostEstimate(
-            flops=2 * 10 * blocks * width**3, bytes_accessed=1 << 20, transcendentals=0
-        ),
+        jax.ShapeDtypeStruct((tokens, own_width), BF16),
+        2 * 10 * blocks * width**3,
+        1 << 20,
     )(gathered, features)
-    grad_skew = pl.pallas_call(
-        sum_kernel,
-        out_shape=jax.ShapeDtypeStruct((blocks * rows, width), F32),
-    )(arrived).reshape(blocks, rows, width)
+    grad_skew = jnp.sum(arrived.astype(F32), axis=0).reshape(blocks, rows, width)
     return grad_acts, grad_skew
 
 

time: 81.7 us -> 64 us (0.78)
  starting transfers between devices: 22.3 us -> 35.9 us
  blocking collectives: 13.2 us -> 0 us
  waiting for transfers between devices: 26.5 us -> 16.2 us
  Pallas kernels: 16.2 us -> 7.26 us
  other arithmetic: 0 us -> 1.43 us
    all_to_all x1, waiting for transfers between devices: 16.3 us -> 0.01 us  [body(): lax.all_to_all(jnp.broadcast_to(packed.reshape(1, blocks * rows, width),...]
    all_to_all x1 -> x0, blocking collectives: 13.2 us -> none  [body(): received = lax.all_to_all(partial, 'outcol', 0, 0, tiled=True)]
    pallas_call x5 -> x4, Pallas kernels: 16.2 us -> 7.26 us  [the longest x1 3.61 us: body(): kernel_call(chain_kernel, jax.ShapeDtypeStruct((shares, blocks * rows, wi...]
    ppermute x0 -> x3, starting transfers between devices: none -> 7.59 us  [body(): lax.ppermute(part, 'outcol', [(i, i ^ turn) for i in range(parts)])]
    all_to_all x1, starting transfers between devices: 6.37 us -> 12.2 us  [body(): arrived = lax.all_to_all(sends, 'dp', 0, 0, tiled=True)]
    ppermute x0 -> x3, waiting for transfers between devices: none -> 4.66 us  [body(): lax.ppermute(part, 'outcol', [(i, i ^ turn) for i in range(parts)])]
    all_to_all x1, waiting for transfers between devices: 10.2 us -> 11.6 us  [body(): arrived = lax.all_to_all(sends, 'dp', 0, 0, tiled=True)]
  transfers between devices with their start and end apart: 2 -> 5, of which waited for: 2 -> 3; matrix products, arithmetic and copies ran while one was open for 0% -> 0% of each run, Pallas kernels for 8% -> 6%
where the time goes in v2:
time: 64 us; the launch traced here: 63.5 us
  starting transfers between devices  35.9 us (56%)
  waiting for transfers between devices  16.2 us (25%)
  Pallas kernels  7.26 us (11%)
  local copies, waits for them, and re-layouts  1.95 us (3%)
  other arithmetic  1.43 us (2%)
  between operations  0.73 us (1%)
    all_to_all x1, starting transfers between devices, body(): lax.all_to_all(jnp.broadcast_to(packed.reshape(1, blocks * rows, width),...  16.1 us
    all_to_all x1, starting transfers between devices, body(): arrived = lax.all_to_all(sends, 'dp', 0, 0, tiled=True)  12.2 us
    all_to_all x1, waiting for transfers between devices, body(): arrived = lax.all_to_all(sends, 'dp', 0, 0, tiled=True)  11.6 us
    ppermute x3, starting transfers between devices, body(): lax.ppermute(part, 'outcol', [(i, i ^ turn) for i in range(parts)])  7.59 us
    ppermute x3, waiting for transfers between devices, body(): lax.ppermute(part, 'outcol', [(i, i ^ turn) for i in range(parts)])  4.66 us
    pallas_call x1, Pallas kernels, body(): kernel_call(chain_kernel, jax.ShapeDtypeStruct((shares, blocks * rows, wi...  3.61 us
    pallas_call x1, Pallas kernels, body(): kernel_call(acts_kernel, jax.ShapeDtypeStruct((tokens, own_width), BF16),...  2.9 us
  transfers between devices with their start and end apart: 5, of which 3 were waited for; matrix products, arithmetic and copies ran while one was open for 0% of the time, Pallas kernels for 6%

profile of v2, /device:TPU:6, one launch (start us, length us, event | category | flops | bytes accessed | tf_op | source)
XLA Modules:
  0.0 63.5 jit_solution(9630582720651772299)
XLA Ops:
  0.6 0.7 %fusion = f16[16,256]{1,0:T(8,128)(2,1)S(1)} fusion(f32[2,8,256]{2,1,0:T(8,128)} %param.7), kind=kLoop, calls=%fused_computation.3 | loop fusion | flops 8192 | bytes 24576 | tf_op jit(solution)/shard_map/broadcast_in_dim | solution.py:116
  1.4 0.7 %broadcast_in_dim.8 = f16[32,16,256]{2,1,0:T(8,128)(2,1)} broadcast(f16[16,256]{1,0:T(8,128)(2,1)S(1)} %fusion), dimensions={1,2} | broadcast | bytes 270336 | tf_op jit(solution)/shard_map/broadcast_in_dim | solution.py:116
  2.1 0.0 copy-start.2
  2.1 16.1 %all-to-all-start = ((f16[32,16,256]{2,1,0:T(8,128)(2,1)}), f16[32,16,256]{2,1,0:T(8,128)(2,1)S(1)}, u32[]{:S(2)}, u32[]{:S(2)}) async-start(f16[32,16,256]{2,1,0:T(8,128)(2,1)} %broadcast_in_dim.8), calls=%async_computation | async-start | bytes 524288 | tf_op jit(solution)/shard_map/all_to_all | solution.py:115
  18.2 0.0 copy-done.2
  18.2 0.0 copy-start
  18.2 1.2 %copy-done = bf16[2048,256]{1,0:T(8,128)(2,1)S(1)} copy-done((bf16[2048,256]{1,0:T(8,128)(2,1)S(1)}, bf16[2048,256]{1,0:T(8,128)(2,1)}, u32[]{:S(2)}) %copy-start) | copy-done | bytes 1048600
  19.4 0.0 copy-start.1
  19.4 0.5 shard_map.59
  19.9 1.9 %collective-permute-start = (bf16[128,512]{1,0:T(8,128)(2,1)S(1)}, bf16[128,512]{1,0:T(8,128)(2,1)S(1)}, u32[]{:S(2)}, u32[]{:S(2)}) collective-permute-start(bf16[128,512]{1,0:T(8,128)(2,1)S(1)} %get-tuple-element.9), channel_id=1, source_target_pairs={{0,1},{1,0},{2,3},{3,2},{4,5},{5,4},{6,7},{7,6},{8,9},{9,8},{10,11... | collective-permute-start | bytes 393224 | tf_op jit(solution)/shard_map/ppermute | solution.py:131
  21.8 2.6 %collective-permute-start.1 = (bf16[128,512]{1,0:T(8,128)(2,1)S(1)}, bf16[128,512]{1,0:T(8,128)(2,1)S(1)}, u32[]{:S(2)}, u32[]{:S(2)}) collective-permute-start(bf16[128,512]{1,0:T(8,128)(2,1)S(1)} %get-tuple-element.10), channel_id=1, source_target_pairs={{0,2},{1,3},{2,0},{3,1},{4,6},{5,7},{6,4},{7,5},{8,10},{9,11},{10,... | collective-permute-start | bytes 393224 | tf_op jit(solution)/shard_map/ppermute | solution.py:131
  24.4 3.1 %collective-permute-start.2 = (bf16[128,512]{1,0:T(8,128)(2,1)S(1)}, bf16[128,512]{1,0:T(8,128)(2,1)S(1)}, u32[]{:S(2)}, u32[]{:S(2)}) collective-permute-start(bf16[128,512]{1,0:T(8,128)(2,1)S(1)} %get-tuple-element.11), channel_id=1, source_target_pairs={{0,3},{1,2},{2,1},{3,0},{4,7},{5,6},{6,5},{7,4},{8,11},{9,10},{10,... | collective-permute-start | bytes 393224 | tf_op jit(solution)/shard_map/ppermute | solution.py:131
  27.5 0.0 collective-permute-done.refs_0_
  27.5 2.4 %collective-permute-done.1.refs_1_ = bf16[128,512]{1,0:T(8,128)(2,1)S(1)} collective-permute-done((bf16[128,512]{1,0:T(8,128)(2,1)S(1)}, bf16[128,512]{1,0:T(8,128)(2,1)S(1)}, u32[]{:S(2)}, u32[]{:S(2)}) %collective-permute-start.1) | collective-permute-done | bytes 131104 | tf_op jit(solution)/shard_map/ppermute | solution.py:131
  29.9 2.3 %collective-permute-done.2.refs_2_ = bf16[128,512]{1,0:T(8,128)(2,1)S(1)} collective-permute-done((bf16[128,512]{1,0:T(8,128)(2,1)S(1)}, bf16[128,512]{1,0:T(8,128)(2,1)S(1)}, u32[]{:S(2)}, u32[]{:S(2)}) %collective-permute-start.2) | collective-permute-done | bytes 131104 | tf_op jit(solution)/shard_map/ppermute | solution.py:131
  32.2 0.0 copy-done.1
  32.2 0.3 shard_map.60
  32.5 0.0 all-to-all-done
  32.5 0.1 multiply_bitcast_fusion.gathered_ref
  32.5 3.6 %shard_map.62 = bf16[32,16,256]{2,1,0:T(8,128)(2,1)} custom-call(f32[32,2,8,256]{3,2,1,0:T(8,128)S(1)} %multiply_bitcast_fusion.gathered_ref, f32[2,256,256]{2,1,0:T(8,128)S(1)} %get-tuple-element.13.grad_ref), custom_call_target="tpu_custom_call" | custom-call | flops 1207959552 | bytes 2097152 | tf_op jit(solution)/shard_map/pallas_call | solution.py:143
  36.1 12.2 %all-to-all-start.1 = ((bf16[32,16,256]{2,1,0:T(8,128)(2,1)}), bf16[32,16,256]{2,1,0:T(8,128)(2,1)S(1)}, u32[]{:S(2)}, u32[]{:S(2)}) async-start(bf16[32,16,256]{2,1,0:T(8,128)(2,1)} %shard_map.62), calls=%async_computation.1 | async-start | bytes 524288 | tf_op jit(solution)/shard_map/all_to_all | solution.py:149
  48.3 2.9 %shard_map.61 = bf16[128,512]{1,0:T(8,128)(2,1)} custom-call(f32[32,2,8,256]{3,2,1,0:T(8,128)S(1)} %multiply_bitcast_fusion.gathered_ref, bf16[128,512]{1,0:T(8,128)(2,1)S(1)} %get-tuple-element.12.features_ref), custom_call_target="tpu_custom_call" | custom-call | flops 671088640 | bytes 1048576 | tf_op jit(solution)/shard_map/pallas_call | solution.py:150
  51.2 11.6 %all-to-all-done.1 = bf16[32,16,256]{2,1,0:T(8,128)(2,1)S(1)} async-done(((bf16[32,16,256]{2,1,0:T(8,128)(2,1)}), bf16[32,16,256]{2,1,0:T(8,128)(2,1)S(1)}, u32[]{:S(2)}, u32[]{:S(2)}) %all-to-all-start.1) | async-done | bytes 262176 | tf_op jit(solution)/shard_map/all_to_all | solution.py:149
  62.8 0.7 %convert_reduce_fusion = f32[16,256]{1,0:T(8,128)} fusion(bf16[32,16,256]{2,1,0:T(8,128)(2,1)S(1)} %all-to-all-done.1), kind=kLoop, calls=%fused_computation | loop fusion | flops 258048 | bytes 278528 | tf_op jit(solution)/shard_map/reduce_sum | solution.py:156
Async XLA Ops:
  2.1 16.1 %copy-start.2 = (bf16[128,256]{1,0:T(8,128)(2,1)S(1)}, bf16[128,256]{1,0:T(8,128)(2,1)}, u32[]{:S(2)}) copy-start(bf16[128,256]{1,0:T(8,128)(2,1)} %cotangent_ref.1) | copy-start | bytes 196612
  2.1 30.4 %all-to-all-start = ((f16[32,16,256]{2,1,0:T(8,128)(2,1)}), f16[32,16,256]{2,1,0:T(8,128)(2,1)S(1)}, u32[]{:S(2)}, u32[]{:S(2)}) async-start(f16[32,16,256]{2,1,0:T(8,128)(2,1)} %broadcast_in_dim.8), calls=%async_computation | async-start | bytes 524288 | tf_op jit(solution)/shard_map/all_to_all | solution.py:115
  18.2 1.2 %copy-start = (bf16[2048,256]{1,0:T(8,128)(2,1)S(1)}, bf16[2048,256]{1,0:T(8,128)(2,1)}, u32[]{:S(2)}) copy-start(bf16[2048,256]{1,0:T(8,128)(2,1)} %weight_ref.1) | copy-start | bytes 3145732
  19.4 12.8 %copy-start.1 = (bf16[128,512]{1,0:T(8,128)(2,1)S(1)}, bf16[128,512]{1,0:T(8,128)(2,1)}, u32[]{:S(2)}) copy-start(bf16[128,512]{1,0:T(8,128)(2,1)} %acts_ref.1) | copy-start | bytes 393220
  19.9 7.6 %collective-permute-start = (bf16[128,512]{1,0:T(8,128)(2,1)S(1)}, bf16[128,512]{1,0:T(8,128)(2,1)S(1)}, u32[]{:S(2)}, u32[]{:S(2)}) collective-permute-start(bf16[128,512]{1,0:T(8,128)(2,1)S(1)} %get-tuple-element.9), channel_id=1, source_target_pairs={{0,1},{1,0},{2,3},{3,2},{4,5},{5,4},{6,7},{7,6},{8,9},{9,8},{10,11... | collective-permute-start | bytes 393224 | tf_op jit(solution)/shard_map/ppermute | solution.py:131
  21.8 8.0 %collective-permute-start.1 = (bf16[128,512]{1,0:T(8,128)(2,1)S(1)}, bf16[128,512]{1,0:T(8,128)(2,1)S(1)}, u32[]{:S(2)}, u32[]{:S(2)}) collective-permute-start(bf16[128,512]{1,0:T(8,128)(2,1)S(1)} %get-tuple-element.10), channel_id=1, source_target_pairs={{0,2},{1,3},{2,0},{3,1},{4,6},{5,7},{6,4},{7,5},{8,10},{9,11},{10,... | collective-permute-start | bytes 393224 | tf_op jit(solution)/shard_map/ppermute | solution.py:131
  24.4 7.8 %collective-permute-start.2 = (bf16[128,512]{1,0:T(8,128)(2,1)S(1)}, bf16[128,512]{1,0:T(8,128)(2,1)S(1)}, u32[]{:S(2)}, u32[]{:S(2)}) collective-permute-start(bf16[128,512]{1,0:T(8,128)(2,1)S(1)} %get-tuple-element.11), channel_id=1, source_target_pairs={{0,3},{1,2},{2,1},{3,0},{4,7},{5,6},{6,5},{7,4},{8,11},{9,10},{10,... | collective-permute-start | bytes 393224 | tf_op jit(solution)/shard_map/ppermute | solution.py:131
  36.1 26.7 %all-to-all-start.1 = ((bf16[32,16,256]{2,1,0:T(8,128)(2,1)}), bf16[32,16,256]{2,1,0:T(8,128)(2,1)S(1)}, u32[]{:S(2)}, u32[]{:S(2)}) async-start(bf16[32,16,256]{2,1,0:T(8,128)(2,1)} %shard_map.62), calls=%async_computation.1 | async-start | bytes 524288 | tf_op jit(solution)/shard_map/all_to_all | solution.py:149

commit v3 on v2

--- a/solution.py
+++ b/solution.py
@@ -30,14 +30,23 @@
     return skew, skew_pair, square, square_pair, square + fourth
 
 
-def features_kernel(cotangent_ref, weight_ref, own_ref, *sent_refs):
+def features_kernel(cotangent_ref, weight_ref, own_ref, *refs):
+    sent_refs, held, semaphores = refs[:-2], refs[-2], refs[-1]
     width = own_ref.shape[1]
     me = lax.axis_index("outcol")
-    for turn in range(1 + len(sent_refs)):
+    turns = range(len(sent_refs), -1, -1)
+    copies = {}
+    for turn in turns:
         first = pl.multiple_of((me ^ turn) * width, width)
+        copies[turn] = pltpu.make_async_copy(
+            weight_ref.at[pl.ds(first, width), :], held.at[turn], semaphores.at[turn]
+        )
+        copies[turn].start()
+    for turn in turns:
+        copies[turn].wait()
         part = lax.dot_general(
             cotangent_ref[...],
-            weight_ref[pl.ds(first, width), :],
+            held[turn],
             (((1,), (1,)), ((), ())),
             preferred_element_type=F32,
         )
@@ -65,18 +74,24 @@
 
 def chain_kernel(gathered_ref, grad_ref, out_ref):
     shares, blocks, rows, width = gathered_ref.shape
-    pieces = []
-    for block in range(blocks):
-        skew, skew_pair, square, square_pair, rest = factors(gathered_ref, block)
-        grad = grad_ref[block]
-        grad_pair = split(grad)
-        left_bar = grad + product(grad_pair, split(rest))
-        right_bar = grad + product(split(square - 2.0 * skew), grad_pair)
-        right_sym = right_bar + right_bar.T
-        both = left_bar + product(split(right_sym), square_pair)
-        square_sym = right_sym + both + both.T
-        total = 2.0 * left_bar - product(split(square_sym), skew_pair)
-        pieces.append((total - total.T).reshape(shares, rows, width))
+    every = range(blocks)
+    param = [gathered_ref[:, b].reshape(width, width) for b in every]
+    skew = [param[b] - param[b].T for b in every]
+    skew_pair = [split(skew[b]) for b in every]
+    square = [product(skew_pair[b], skew_pair[b]) for b in every]
+    square_pair = [split(square[b]) for b in every]
+    grad = [grad_ref[b] for b in every]
+    grad_pair = [split(grad[b]) for b in every]
+    right_bar = [
+        grad[b] + product(split(square[b] - 2.0 * skew[b]), grad_pair[b]) for b in every
+    ]
+    fourth = [product(square_pair[b], square_pair[b]) for b in every]
+    left_bar = [grad[b] + product(grad_pair[b], split(square[b] + fourth[b])) for b in every]
+    right_sym = [right_bar[b] + right_bar[b].T for b in every]
+    both = [left_bar[b] + product(split(right_sym[b]), square_pair[b]) for b in every]
+    square_sym = [right_sym[b] + both[b] + both[b].T for b in every]
+    total = [2.0 * left_bar[b] - product(split(square_sym[b]), skew_pair[b]) for b in every]
+    pieces = [(total[b] - total[b].T).reshape(shares, rows, width) for b in every]
     out_ref[...] = jnp.concatenate(pieces, axis=1).astype(BF16)
 
 
@@ -95,12 +110,13 @@
         ).astype(BF16)
 
 
-def kernel_call(kernel, out_shape, flops, moved):
+def kernel_call(kernel, out_shape, flops, moved, **specs):
     return pl.pallas_call(
         kernel,
         out_shape=out_shape,
         compiler_params=pltpu.CompilerParams(vmem_limit_bytes=24 << 20),
         cost_estimate=pl.CostEstimate(flops=flops, bytes_accessed=moved, transcendentals=0),
+        **specs,
     )
 
 
@@ -111,13 +127,9 @@
     depth = cotangent.shape[1]
     blocks, rows, width = skew_param.shape
     scale = 65536.0
-    packed = (skew_param * scale).astype(jnp.float16)
+    packed = (skew_param * scale).astype(jnp.float16).reshape(1, blocks * rows, width)
     gathered = lax.all_to_all(
-        jnp.broadcast_to(packed.reshape(1, blocks * rows, width), (shares, blocks * rows, width)),
-        "dp",
-        0,
-        0,
-        tiled=True,
+        jnp.broadcast_to(packed, (shares, blocks * rows, width)), "dp", 0, 0, tiled=True
     )
     gathered = (gathered.astype(F32) * (1.0 / scale)).reshape(shares, blocks, rows, width)
     own, *sent = kernel_call(
@@ -126,10 +138,15 @@
         + [jax.ShapeDtypeStruct((tokens, own_width), BF16)] * (parts - 1),
         2 * tokens * depth * own_width * parts,
         2 << 20,
-    )(cotangent, base_weight)
+        in_specs=[pl.BlockSpec(memory_space=pltpu.VMEM), pl.BlockSpec(memory_space=pltpu.HBM)],
+        scratch_shapes=[
+            pltpu.VMEM((parts, own_width, depth), BF16),
+            pltpu.SemaphoreType.DMA((parts,)),
+        ],
+    )(cotangent, pltpu.with_memory_space_constraint(base_weight, pltpu.HBM))
     received = [
-        lax.ppermute(part, "outcol", [(i, i ^ turn) for i in range(parts)])
-        for turn, part in enumerate(sent, 1)
+        lax.ppermute(sent[turn - 1], "outcol", [(i, i ^ turn) for i in range(parts)])
+        for turn in range(parts - 1, 0, -1)
     ]
     features, grad_rot = kernel_call(
         block_grad_kernel,

time: 64 us -> 61.2 us (0.956)
  starting transfers between devices: 35.9 us -> 34 us
  local copies, waits for them, and re-layouts: 1.95 us -> 0.73 us
  Pallas kernels: 7.26 us -> 7.99 us
    all_to_all x1, starting transfers between devices: 12.2 us -> 10.3 us  [body(): arrived = lax.all_to_all(sends, 'dp', 0, 0, tiled=True)]
    ppermute x3, waiting for transfers between devices: 4.66 us -> 3.17 us  [body(): lax.ppermute(sent[turn - 1], 'outcol', [(i, i ^ turn) for i in range(part...]
    pallas_call x1, Pallas kernels: 0.48 us -> 1.93 us  [body(): kernel_call(features_kernel, [jax.ShapeDtypeStruct((tokens, own_width), F...]
    all_to_all x1, waiting for transfers between devices: 0.01 us -> 1.22 us  [body(): lax.all_to_all(jnp.broadcast_to(packed, (shares, blocks * rows, width)),...]
    unnamed x6 -> x4, local copies, waits for them, and re-layouts: 1.23 us -> 0.01 us
    pallas_call x1, Pallas kernels: 3.61 us -> 2.89 us  [body(): kernel_call(chain_kernel, jax.ShapeDtypeStruct((shares, blocks * rows, wi...]
  transfers between devices with their start and end apart: 5 -> 5, of which waited for: 3 -> 4; matrix products, arithmetic and copies ran while one was open for 0% -> 0% of each run, Pallas kernels for 6% -> 8%
where the time goes in v3:
time: 61.2 us; the launch traced here: 60.8 us
  starting transfers between devices  34 us (56%)
  waiting for transfers between devices  15.9 us (26%)
  Pallas kernels  7.99 us (13%)
  other arithmetic  1.43 us (2%)
  local copies, waits for them, and re-layouts  0.73 us (1%)
  between operations  0.71 us (1%)
    all_to_all x1, starting transfers between devices, body(): lax.all_to_all(jnp.broadcast_to(packed, (shares, blocks * rows, width)),...  16.1 us
    all_to_all x1, waiting for transfers between devices, body(): arrived = lax.all_to_all(sends, 'dp', 0, 0, tiled=True)  11.5 us
    all_to_all x1, starting transfers between devices, body(): arrived = lax.all_to_all(sends, 'dp', 0, 0, tiled=True)  10.3 us
    ppermute x3, starting transfers between devices, body(): lax.ppermute(sent[turn - 1], 'outcol', [(i, i ^ turn) for i in range(part...  7.59 us
    ppermute x3, waiting for transfers between devices, body(): lax.ppermute(sent[turn - 1], 'outcol', [(i, i ^ turn) for i in range(part...  3.17 us
    pallas_call x1, Pallas kernels, body(): kernel_call(acts_kernel, jax.ShapeDtypeStruct((tokens, own_width), BF16),...  2.9 us
    pallas_call x1, Pallas kernels, body(): kernel_call(chain_kernel, jax.ShapeDtypeStruct((shares, blocks * rows, wi...  2.89 us
    pallas_call x1, Pallas kernels, body(): kernel_call(features_kernel, [jax.ShapeDtypeStruct((tokens, own_width), F...  1.93 us
  transfers between devices with their start and end apart: 5, of which 4 were waited for; matrix products, arithmetic and copies ran while one was open for 0% of the time, Pallas kernels for 8%

profile of v3, /device:TPU:6, one launch (start us, length us, event | category | flops | bytes accessed | tf_op | source)
XLA Modules:
  0.0 60.8 jit_solution(11115853926285199406)
XLA Ops:
  0.6 0.7 %fusion = f16[16,256]{1,0:T(8,128)(2,1)S(1)} fusion(f32[2,8,256]{2,1,0:T(8,128)} %param.7), kind=kLoop, calls=%fused_computation.3 | loop fusion | flops 8192 | bytes 24576 | tf_op jit(solution)/shard_map/broadcast_in_dim | solution.py:132
  1.4 0.7 %broadcast_in_dim.8 = f16[32,16,256]{2,1,0:T(8,128)(2,1)} broadcast(f16[16,256]{1,0:T(8,128)(2,1)S(1)} %fusion), dimensions={1,2} | broadcast | bytes 270336 | tf_op jit(solution)/shard_map/broadcast_in_dim | solution.py:132
  2.1 0.0 copy-start.1
  2.1 16.1 %all-to-all-start = ((f16[32,16,256]{2,1,0:T(8,128)(2,1)}), f16[32,16,256]{2,1,0:T(8,128)(2,1)S(1)}, u32[]{:S(2)}, u32[]{:S(2)}) async-start(f16[32,16,256]{2,1,0:T(8,128)(2,1)} %broadcast_in_dim.8), calls=%async_computation | async-start | bytes 524288 | tf_op jit(solution)/shard_map/all_to_all | solution.py:131
  18.2 0.0 copy-done.1
  18.2 0.0 copy-start
  18.2 1.9 %shard_map.59 = (f32[128,512]{1,0:T(8,128)S(1)}, bf16[128,512]{1,0:T(8,128)(2,1)S(1)}, bf16[128,512]{1,0:T(8,128)(2,1)S(1)}, bf16[128,512]{1,0:T(8,128)(2,1)S(1)}) custom-call(bf16[128,256]{1,0:T(8,128)(2,1)S(1)} %copy-done.1, bf16[2048,256]{1,0:T(8,128)(2,1)} %weight_ref.1), custom_call_target="tpu_custom_call" | custom-call | flops 134217728 | bytes 2097152 | tf_op jit(solution)/shard_map/pallas_call | solution.py:135
  20.1 1.9 %collective-permute-start = (bf16[128,512]{1,0:T(8,128)(2,1)S(1)}, bf16[128,512]{1,0:T(8,128)(2,1)S(1)}, u32[]{:S(2)}, u32[]{:S(2)}) collective-permute-start(bf16[128,512]{1,0:T(8,128)(2,1)S(1)} %get-tuple-element.9), channel_id=1, source_target_pairs={{0,3},{1,2},{2,1},{3,0},{4,7},{5,6},{6,5},{7,4},{8,11},{9,10},{10,... | collective-permute-start | bytes 393224 | tf_op jit(solution)/shard_map/ppermute | solution.py:148
  22.1 3.1 %collective-permute-start.1 = (bf16[128,512]{1,0:T(8,128)(2,1)S(1)}, bf16[128,512]{1,0:T(8,128)(2,1)S(1)}, u32[]{:S(2)}, u32[]{:S(2)}) collective-permute-start(bf16[128,512]{1,0:T(8,128)(2,1)S(1)} %get-tuple-element.10), channel_id=1, source_target_pairs={{0,2},{1,3},{2,0},{3,1},{4,6},{5,7},{6,4},{7,5},{8,10},{9,11},{10,... | collective-permute-start | bytes 393224 | tf_op jit(solution)/shard_map/ppermute | solution.py:148
  25.2 2.6 %collective-permute-start.2 = (bf16[128,512]{1,0:T(8,128)(2,1)S(1)}, bf16[128,512]{1,0:T(8,128)(2,1)S(1)}, u32[]{:S(2)}, u32[]{:S(2)}) collective-permute-start(bf16[128,512]{1,0:T(8,128)(2,1)S(1)} %get-tuple-element.11), channel_id=1, source_target_pairs={{0,1},{1,0},{2,3},{3,2},{4,5},{5,4},{6,7},{7,6},{8,9},{9,8},{10,11... | collective-permute-start | bytes 393224 | tf_op jit(solution)/shard_map/ppermute | solution.py:148
  27.8 0.6 %collective-permute-done.refs_0_ = bf16[128,512]{1,0:T(8,128)(2,1)S(1)} collective-permute-done((bf16[128,512]{1,0:T(8,128)(2,1)S(1)}, bf16[128,512]{1,0:T(8,128)(2,1)S(1)}, u32[]{:S(2)}, u32[]{:S(2)}) %collective-permute-start) | collective-permute-done | bytes 131104 | tf_op jit(solution)/shard_map/ppermute | solution.py:148
  28.4 2.5 %collective-permute-done.1.refs_1_ = bf16[128,512]{1,0:T(8,128)(2,1)S(1)} collective-permute-done((bf16[128,512]{1,0:T(8,128)(2,1)S(1)}, bf16[128,512]{1,0:T(8,128)(2,1)S(1)}, u32[]{:S(2)}, u32[]{:S(2)}) %collective-permute-start.1) | collective-permute-done | bytes 131104 | tf_op jit(solution)/shard_map/ppermute | solution.py:148
  30.9 0.0 collective-permute-done.2.refs_2_
  30.9 0.0 copy-done
  30.9 0.3 shard_map.60
  31.2 1.2 %all-to-all-done = f16[32,16,256]{2,1,0:T(8,128)(2,1)S(1)} async-done(((f16[32,16,256]{2,1,0:T(8,128)(2,1)}), f16[32,16,256]{2,1,0:T(8,128)(2,1)S(1)}, u32[]{:S(2)}, u32[]{:S(2)}) %all-to-all-start) | async-done | bytes 262176 | tf_op jit(solution)/shard_map/all_to_all | solution.py:131
  32.4 0.1 multiply_bitcast_fusion.gathered_ref
  32.5 2.9 %shard_map.62 = bf16[32,16,256]{2,1,0:T(8,128)(2,1)} custom-call(f32[32,2,8,256]{3,2,1,0:T(8,128)S(1)} %multiply_bitcast_fusion.gathered_ref, f32[2,256,256]{2,1,0:T(8,128)S(1)} %get-tuple-element.13.grad_ref), custom_call_target="tpu_custom_call" | custom-call | flops 1207959552 | bytes 2097152 | tf_op jit(solution)/shard_map/pallas_call | solution.py:160
  35.4 10.3 %all-to-all-start.1 = ((bf16[32,16,256]{2,1,0:T(8,128)(2,1)}), bf16[32,16,256]{2,1,0:T(8,128)(2,1)S(1)}, u32[]{:S(2)}, u32[]{:S(2)}) async-start(bf16[32,16,256]{2,1,0:T(8,128)(2,1)} %shard_map.62), calls=%async_computation.1 | async-start | bytes 524288 | tf_op jit(solution)/shard_map/all_to_all | solution.py:166
  45.7 2.9 %shard_map.61 = bf16[128,512]{1,0:T(8,128)(2,1)} custom-call(f32[32,2,8,256]{3,2,1,0:T(8,128)S(1)} %multiply_bitcast_fusion.gathered_ref, bf16[128,512]{1,0:T(8,128)(2,1)S(1)} %get-tuple-element.12.features_ref), custom_call_target="tpu_custom_call" | custom-call | flops 671088640 | bytes 1048576 | tf_op jit(solution)/shard_map/pallas_call | solution.py:167
  48.6 11.5 %all-to-all-done.1 = bf16[32,16,256]{2,1,0:T(8,128)(2,1)S(1)} async-done(((bf16[32,16,256]{2,1,0:T(8,128)(2,1)}), bf16[32,16,256]{2,1,0:T(8,128)(2,1)S(1)}, u32[]{:S(2)}, u32[]{:S(2)}) %all-to-all-start.1) | async-done | bytes 262176 | tf_op jit(solution)/shard_map/all_to_all | solution.py:166
  60.1 0.7 %convert_reduce_fusion = f32[16,256]{1,0:T(8,128)} fusion(bf16[32,16,256]{2,1,0:T(8,128)(2,1)S(1)} %all-to-all-done.1), kind=kLoop, calls=%fused_computation | loop fusion | flops 258048 | bytes 278528 | tf_op jit(solution)/shard_map/reduce_sum | solution.py:173
Async XLA Ops:
  2.1 16.1 %copy-start.1 = (bf16[128,256]{1,0:T(8,128)(2,1)S(1)}, bf16[128,256]{1,0:T(8,128)(2,1)}, u32[]{:S(2)}) copy-start(bf16[128,256]{1,0:T(8,128)(2,1)} %cotangent_ref.1) | copy-start | bytes 196612
  2.1 30.3 %all-to-all-start = ((f16[32,16,256]{2,1,0:T(8,128)(2,1)}), f16[32,16,256]{2,1,0:T(8,128)(2,1)S(1)}, u32[]{:S(2)}, u32[]{:S(2)}) async-start(f16[32,16,256]{2,1,0:T(8,128)(2,1)} %broadcast_in_dim.8), calls=%async_computation | async-start | bytes 524288 | tf_op jit(solution)/shard_map/all_to_all | solution.py:131
  18.2 12.7 %copy-start = (bf16[128,512]{1,0:T(8,128)(2,1)S(1)}, bf16[128,512]{1,0:T(8,128)(2,1)}, u32[]{:S(2)}) copy-start(bf16[128,512]{1,0:T(8,128)(2,1)} %acts_ref.1) | copy-start | bytes 393220
  20.1 8.2 %collective-permute-start = (bf16[128,512]{1,0:T(8,128)(2,1)S(1)}, bf16[128,512]{1,0:T(8,128)(2,1)S(1)}, u32[]{:S(2)}, u32[]{:S(2)}) collective-permute-start(bf16[128,512]{1,0:T(8,128)(2,1)S(1)} %get-tuple-element.9), channel_id=1, source_target_pairs={{0,3},{1,2},{2,1},{3,0},{4,7},{5,6},{6,5},{7,4},{8,11},{9,10},{10,... | collective-permute-start | bytes 393224 | tf_op jit(solution)/shard_map/ppermute | solution.py:148
  22.1 8.9 %collective-permute-start.1 = (bf16[128,512]{1,0:T(8,128)(2,1)S(1)}, bf16[128,512]{1,0:T(8,128)(2,1)S(1)}, u32[]{:S(2)}, u32[]{:S(2)}) collective-permute-start(bf16[128,512]{1,0:T(8,128)(2,1)S(1)} %get-tuple-element.10), channel_id=1, source_target_pairs={{0,2},{1,3},{2,0},{3,1},{4,6},{5,7},{6,4},{7,5},{8,10},{9,11},{10,... | collective-permute-start | bytes 393224 | tf_op jit(solution)/shard_map/ppermute | solution.py:148
  25.2 5.8 %collective-permute-start.2 = (bf16[128,512]{1,0:T(8,128)(2,1)S(1)}, bf16[128,512]{1,0:T(8,128)(2,1)S(1)}, u32[]{:S(2)}, u32[]{:S(2)}) collective-permute-start(bf16[128,512]{1,0:T(8,128)(2,1)S(1)} %get-tuple-element.11), channel_id=1, source_target_pairs={{0,1},{1,0},{2,3},{3,2},{4,5},{5,4},{6,7},{7,6},{8,9},{9,8},{10,11... | collective-permute-start | bytes 393224 | tf_op jit(solution)/shard_map/ppermute | solution.py:148
  35.4 24.7 %all-to-all-start.1 = ((bf16[32,16,256]{2,1,0:T(8,128)(2,1)}), bf16[32,16,256]{2,1,0:T(8,128)(2,1)S(1)}, u32[]{:S(2)}, u32[]{:S(2)}) async-start(bf16[32,16,256]{2,1,0:T(8,128)(2,1)} %shard_map.62), calls=%async_computation.1 | async-start | bytes 524288 | tf_op jit(solution)/shard_map/all_to_all | solution.py:166

commit v4 on v3

--- a/solution.py
+++ b/solution.py
@@ -30,39 +30,41 @@
     return skew, skew_pair, square, square_pair, square + fourth
 
 
-def features_kernel(cotangent_ref, weight_ref, own_ref, *refs):
-    sent_refs, held, semaphores = refs[:-2], refs[-2], refs[-1]
-    width = own_ref.shape[1]
-    me = lax.axis_index("outcol")
-    turns = range(len(sent_refs), -1, -1)
-    copies = {}
-    for turn in turns:
-        first = pl.multiple_of((me ^ turn) * width, width)
-        copies[turn] = pltpu.make_async_copy(
-            weight_ref.at[pl.ds(first, width), :], held.at[turn], semaphores.at[turn]
-        )
-        copies[turn].start()
-    for turn in turns:
-        copies[turn].wait()
-        part = lax.dot_general(
-            cotangent_ref[...],
-            held[turn],
-            (((1,), (1,)), ((), ())),
-            preferred_element_type=F32,
-        )
-        if turn:
-            sent_refs[turn - 1][...] = part.astype(BF16)
-        else:
-            own_ref[...] = part
+def partial_sum(cotangent, weight):
+    return lax.dot_general(
+        cotangent, weight, (((1,), (1,)), ((), ())), preferred_element_type=F32
+    )
 
 
-def block_grad_kernel(acts_ref, own_ref, *refs):
-    part_refs, (features_ref, grad_ref) = refs[:-2], refs[-2:]
+def sent_kernel(cotangent_ref, weight_ref, out_ref, held, semaphores):
+    width = out_ref.shape[-1]
+    partner = lax.axis_index("outcol") ^ 1
+    copies = []
+    for half in range(out_ref.shape[0]):
+        first = pl.multiple_of((partner ^ (2 * half)) * width, width)
+        copies.append(
+            pltpu.make_async_copy(
+                weight_ref.at[pl.ds(first, width), :], held.at[half], semaphores.at[half]
+            )
+        )
+        copies[half].start()
+    for half in range(out_ref.shape[0]):
+        copies[half].wait()
+        out_ref[half] = partial_sum(cotangent_ref[...], held[half]).astype(BF16)
+
+
+def kept_kernel(cotangent_ref, weight_ref, other_ref, own_ref, sent_ref):
+    width = own_ref.shape[-1]
+    me = lax.axis_index("outcol")
+    for half, out_ref in ((1, sent_ref), (0, own_ref)):
+        first = pl.multiple_of((me ^ (2 * half)) * width, width)
+        part = partial_sum(cotangent_ref[...], weight_ref[pl.ds(first, width), :])
+        out_ref[...] = (part + other_ref[half].astype(F32)).astype(out_ref.dtype)
+
+
+def block_grad_kernel(acts_ref, own_ref, other_ref, features_ref, grad_ref):
     blocks, width = grad_ref.shape[0], grad_ref.shape[-1]
-    total = own_ref[...]
-    for part_ref in part_refs:
-        total = total + part_ref[...].astype(F32)
-    features = total.astype(BF16)
+    features = (own_ref[...] + other_ref[...].astype(F32)).astype(BF16)
     features_ref[...] = features
     acts = acts_ref[...]
     for block in range(blocks):
@@ -127,27 +129,35 @@
     depth = cotangent.shape[1]
     blocks, rows, width = skew_param.shape
     scale = 65536.0
-    packed = (skew_param * scale).astype(jnp.float16).reshape(1, blocks * rows, width)
-    gathered = lax.all_to_all(
-        jnp.broadcast_to(packed, (shares, blocks * rows, width)), "dp", 0, 0, tiled=True
-    )
+    shape = (shares, blocks * rows, width)
+    place = lax.broadcasted_iota(jnp.int32, shape, 0) + lax.broadcasted_iota(jnp.int32, shape, 2)
+    copies = jnp.where(place < 0, 0.0, skew_param.reshape(1, blocks * rows, width)) * scale
+    gathered = lax.all_to_all(copies.astype(jnp.float16), "dp", 0, 0, tiled=True)
     gathered = (gathered.astype(F32) * (1.0 / scale)).reshape(shares, blocks, rows, width)
-    own, *sent = kernel_call(
-        features_kernel,
-        [jax.ShapeDtypeStruct((tokens, own_width), F32)]
-        + [jax.ShapeDtypeStruct((tokens, own_width), BF16)] * (parts - 1),
-        2 * tokens * depth * own_width * parts,
-        2 << 20,
-        in_specs=[pl.BlockSpec(memory_space=pltpu.VMEM), pl.BlockSpec(memory_space=pltpu.HBM)],
+    vmem = pl.BlockSpec(memory_space=pltpu.VMEM)
+    flops = tokens * depth * own_width * parts
+    to_core = kernel_call(
+        sent_kernel,
+        jax.ShapeDtypeStruct((parts // 2, tokens, own_width), BF16),
+        flops,
+        1 << 20,
+        in_specs=[vmem, pl.BlockSpec(memory_space=pltpu.HBM)],
         scratch_shapes=[
-            pltpu.VMEM((parts, own_width, depth), BF16),
-            pltpu.SemaphoreType.DMA((parts,)),
+            pltpu.VMEM((parts // 2, own_width, depth), BF16),
+            pltpu.SemaphoreType.DMA((parts // 2,)),
         ],
     )(cotangent, pltpu.with_memory_space_constraint(base_weight, pltpu.HBM))
-    received = [
-        lax.ppermute(sent[turn - 1], "outcol", [(i, i ^ turn) for i in range(parts)])
-        for turn in range(parts - 1, 0, -1)
-    ]
+    from_core = lax.ppermute(to_core, "outcol", [(i, i ^ 1) for i in range(parts)])
+    own, to_chip = kernel_call(
+        kept_kernel,
+        (
+            jax.ShapeDtypeStruct((tokens, own_width), F32),
+            jax.ShapeDtypeStruct((tokens, own_width), BF16),
+        ),
+        flops,
+        1 << 20,
+    )(cotangent, base_weight, from_core)
+    received = [lax.ppermute(to_chip, "outcol", [(i, i ^ 2) for i in range(parts)])]
     features, grad_rot = kernel_call(
         block_grad_kernel,
         (

time: 61.2 us -> 62.3 us (1.018)
  waiting for transfers between devices: 15.9 us -> 17.8 us
  starting transfers between devices: 34 us -> 32.4 us
  other arithmetic: 1.43 us -> 2.23 us
    ppermute x3 -> x2, waiting for transfers between devices: 3.17 us -> 6.34 us  [the longest x1 4.83 us: body(): lax.ppermute(to_chip, 'outcol', [(i, i ^ 2) for i in range(parts)])]
    ppermute x3 -> x2, starting transfers between devices: 7.59 us -> 4.64 us  [the longest x1 2.58 us: body(): lax.ppermute(to_chip, 'outcol', [(i, i ^ 2) for i in range(parts)])]
    convert_element_type x0 -> x1, other arithmetic: none -> 1.52 us  [body(): copies.astype(jnp.float16)]
    all_to_all x1, starting transfers between devices: 10.3 us -> 11.8 us  [body(): arrived = lax.all_to_all(sends, 'dp', 0, 0, tiled=True)]
    unnamed x4 -> x6, local copies, waits for them, and re-layouts: 0.01 us -> 0.85 us
    all_to_all x1, waiting for transfers between devices: 1.22 us -> 0.4 us  [body(): lax.all_to_all(copies.astype(jnp.float16), 'dp', 0, 0, tiled=True)]
    broadcast_in_dim x1 -> x0, other arithmetic: 0.72 us -> none  [body(): jnp.broadcast_to(packed, (shares, blocks * rows, width))]
    broadcast_in_dim x1 -> x0, local copies, waits for them, and re-layouts: 0.72 us -> none  [body(): jnp.broadcast_to(packed, (shares, blocks * rows, width))]
  transfers between devices with their start and end apart: 5 -> 4, of which waited for: 4 -> 4; matrix products, arithmetic and copies ran while one was open for 0% -> 0% of each run, Pallas kernels for 8% -> 8%
where the time goes in v4:
time: 62.3 us; the launch traced here: 61.8 us
  starting transfers between devices  32.4 us (52%)
  waiting for transfers between devices  17.8 us (29%)
  Pallas kernels  7.76 us (12%)
  other arithmetic  2.23 us (4%)
  local copies, waits for them, and re-layouts  0.85 us (1%)
  between operations  0.72 us (1%)
    all_to_all x1, starting transfers between devices, body(): lax.all_to_all(copies.astype(jnp.float16), 'dp', 0, 0, tiled=True)  16 us
    all_to_all x1, starting transfers between devices, body(): arrived = lax.all_to_all(sends, 'dp', 0, 0, tiled=True)  11.8 us
    all_to_all x1, waiting for transfers between devices, body(): arrived = lax.all_to_all(sends, 'dp', 0, 0, tiled=True)  11.1 us
    ppermute x1, waiting for transfers between devices, body(): lax.ppermute(to_chip, 'outcol', [(i, i ^ 2) for i in range(parts)])  4.83 us
    pallas_call x1, Pallas kernels, body(): kernel_call(acts_kernel, jax.ShapeDtypeStruct((tokens, own_width), BF16),...  2.9 us
    pallas_call x1, Pallas kernels, body(): kernel_call(chain_kernel, jax.ShapeDtypeStruct((shares, blocks * rows, wi...  2.89 us
    ppermute x1, starting transfers between devices, body(): lax.ppermute(to_chip, 'outcol', [(i, i ^ 2) for i in range(parts)])  2.58 us
    ppermute x1, starting transfers between devices, body(): lax.ppermute(to_core, 'outcol', [(i, i ^ 1) for i in range(parts)])  2.05 us
  transfers between devices with their start and end apart: 4, of which 4 were waited for; matrix products, arithmetic and copies ran while one was open for 0% of the time, Pallas kernels for 8%

profile of v4, /device:TPU:6, one launch (start us, length us, event | category | flops | bytes accessed | tf_op | source)
XLA Modules:
  0.0 61.8 jit_solution(5480392911993726679)
XLA Ops:
  0.6 0.0 copy-start
  0.6 1.5 %multiply_convert_fusion = f16[32,16,256]{2,1,0:T(8,128)(2,1)} fusion(f32[16,256]{1,0:T(8,128)} %bitcast.4), kind=kLoop, calls=%fused_computation.2 | loop fusion | flops 655360 | bytes 278528 | tf_op jit(solution)/shard_map/convert_element_type | solution.py:135
  2.2 16.0 %all-to-all-start = ((f16[32,16,256]{2,1,0:T(8,128)(2,1)}), f16[32,16,256]{2,1,0:T(8,128)(2,1)S(1)}, u32[]{:S(2)}, u32[]{:S(2)}) async-start(f16[32,16,256]{2,1,0:T(8,128)(2,1)} %multiply_convert_fusion), calls=%async_computation | async-start | bytes 524288 | tf_op jit(solution)/shard_map/all_to_all | solution.py:135
  18.1 0.0 copy-start.1
  18.1 0.8 %copy-done.1 = bf16[128,256]{1,0:T(8,128)(2,1)S(1)} copy-done((bf16[128,256]{1,0:T(8,128)(2,1)S(1)}, bf16[128,256]{1,0:T(8,128)(2,1)}, u32[]{:S(2)}) %copy-start.1) | copy-done | bytes 65560
  19.0 1.4 %shard_map.59 = bf16[2,128,512]{2,1,0:T(8,128)(2,1)S(1)} custom-call(bf16[128,256]{1,0:T(8,128)(2,1)S(1)} %copy-done.1, bf16[2048,256]{1,0:T(8,128)(2,1)} %weight_ref.3), custom_call_target="tpu_custom_call" | custom-call | flops 67108864 | bytes 1048576 | tf_op jit(solution)/shard_map/pallas_call | solution.py:139
  20.4 0.0 copy-start.2
  20.4 2.1 %collective-permute-start = (bf16[2,128,512]{2,1,0:T(8,128)(2,1)S(1)}, bf16[2,128,512]{2,1,0:T(8,128)(2,1)S(1)}, u32[]{:S(2)}, u32[]{:S(2)}) collective-permute-start(bf16[2,128,512]{2,1,0:T(8,128)(2,1)S(1)} %shard_map.59), channel_id=1, source_target_pairs={{0,1},{1,0},{2,3},{3,2},{4,5},{5,4},{6,7},{7,6},{8,9},{9,8},{10,11... | collective-permute-start | bytes 786440 | tf_op jit(solution)/shard_map/ppermute | solution.py:150
  22.5 1.5 %collective-permute-done.other_ref = bf16[2,128,512]{2,1,0:T(8,128)(2,1)S(1)} collective-permute-done((bf16[2,128,512]{2,1,0:T(8,128)(2,1)S(1)}, bf16[2,128,512]{2,1,0:T(8,128)(2,1)S(1)}, u32[]{:S(2)}, u32[]{:S(2)}) %collective-permute-start) | collective-permute-done | bytes 262176 | tf_op jit(solution)/shard_map/ppermute | solution.py:150
  24.0 0.0 copy-done
  24.0 0.3 shard_map.60
  24.3 2.6 %collective-permute-start.1 = (bf16[128,512]{1,0:T(8,128)(2,1)S(1)}, bf16[128,512]{1,0:T(8,128)(2,1)S(1)}, u32[]{:S(2)}, u32[]{:S(2)}) collective-permute-start(bf16[128,512]{1,0:T(8,128)(2,1)S(1)} %get-tuple-element.7), channel_id=1, source_target_pairs={{0,2},{1,3},{2,0},{3,1},{4,6},{5,7},{6,4},{7,5},{8,10},{9,11},{10,... | collective-permute-start | bytes 393224 | tf_op jit(solution)/shard_map/ppermute | solution.py:160
  26.9 4.8 %collective-permute-done.1.other_ref = bf16[128,512]{1,0:T(8,128)(2,1)S(1)} collective-permute-done((bf16[128,512]{1,0:T(8,128)(2,1)S(1)}, bf16[128,512]{1,0:T(8,128)(2,1)S(1)}, u32[]{:S(2)}, u32[]{:S(2)}) %collective-permute-start.1) | collective-permute-done | bytes 131104 | tf_op jit(solution)/shard_map/ppermute | solution.py:160
  31.7 0.0 copy-done.2
  31.7 0.2 shard_map.61
  32.0 0.4 all-to-all-done
  32.4 0.1 multiply_bitcast_fusion.gathered_ref
  32.4 2.9 %shard_map.63 = bf16[32,16,256]{2,1,0:T(8,128)(2,1)} custom-call(f32[32,2,8,256]{3,2,1,0:T(8,128)S(1)} %multiply_bitcast_fusion.gathered_ref, f32[2,256,256]{2,1,0:T(8,128)S(1)} %get-tuple-element.9.grad_ref), custom_call_target="tpu_custom_call" | custom-call | flops 1207959552 | bytes 2097152 | tf_op jit(solution)/shard_map/pallas_call | solution.py:170
  35.3 11.8 %all-to-all-start.1 = ((bf16[32,16,256]{2,1,0:T(8,128)(2,1)}), bf16[32,16,256]{2,1,0:T(8,128)(2,1)S(1)}, u32[]{:S(2)}, u32[]{:S(2)}) async-start(bf16[32,16,256]{2,1,0:T(8,128)(2,1)} %shard_map.63), calls=%async_computation.1 | async-start | bytes 524288 | tf_op jit(solution)/shard_map/all_to_all | solution.py:176
  47.1 2.9 %shard_map.62 = bf16[128,512]{1,0:T(8,128)(2,1)} custom-call(f32[32,2,8,256]{3,2,1,0:T(8,128)S(1)} %multiply_bitcast_fusion.gathered_ref, bf16[128,512]{1,0:T(8,128)(2,1)S(1)} %get-tuple-element.8.features_ref), custom_call_target="tpu_custom_call" | custom-call | flops 671088640 | bytes 1048576 | tf_op jit(solution)/shard_map/pallas_call | solution.py:177
  50.0 11.1 %all-to-all-done.1 = bf16[32,16,256]{2,1,0:T(8,128)(2,1)S(1)} async-done(((bf16[32,16,256]{2,1,0:T(8,128)(2,1)}), bf16[32,16,256]{2,1,0:T(8,128)(2,1)S(1)}, u32[]{:S(2)}, u32[]{:S(2)}) %all-to-all-start.1) | async-done | bytes 262176 | tf_op jit(solution)/shard_map/all_to_all | solution.py:176
  61.1 0.7 %convert_reduce_fusion = f32[16,256]{1,0:T(8,128)} fusion(bf16[32,16,256]{2,1,0:T(8,128)(2,1)S(1)} %all-to-all-done.1), kind=kLoop, calls=%fused_computation | loop fusion | flops 258048 | bytes 278528 | tf_op jit(solution)/shard_map/reduce_sum | solution.py:183
Async XLA Ops:
  0.6 23.4 %copy-start = (bf16[2048,256]{1,0:T(8,128)(2,1)S(1)}, bf16[2048,256]{1,0:T(8,128)(2,1)}, u32[]{:S(2)}) copy-start(bf16[2048,256]{1,0:T(8,128)(2,1)} %weight_ref.3) | copy-start | bytes 3145732
  2.2 30.2 %all-to-all-start = ((f16[32,16,256]{2,1,0:T(8,128)(2,1)}), f16[32,16,256]{2,1,0:T(8,128)(2,1)S(1)}, u32[]{:S(2)}, u32[]{:S(2)}) async-start(f16[32,16,256]{2,1,0:T(8,128)(2,1)} %multiply_convert_fusion), calls=%async_computation | async-start | bytes 524288 | tf_op jit(solution)/shard_map/all_to_all | solution.py:135
  18.1 0.8 %copy-start.1 = (bf16[128,256]{1,0:T(8,128)(2,1)S(1)}, bf16[128,256]{1,0:T(8,128)(2,1)}, u32[]{:S(2)}) copy-start(bf16[128,256]{1,0:T(8,128)(2,1)} %cotangent_ref.3) | copy-start | bytes 196612
  20.4 11.3 %copy-start.2 = (bf16[128,512]{1,0:T(8,128)(2,1)S(1)}, bf16[128,512]{1,0:T(8,128)(2,1)}, u32[]{:S(2)}) copy-start(bf16[128,512]{1,0:T(8,128)(2,1)} %acts_ref.1) | copy-start | bytes 393220
  20.4 3.6 %collective-permute-start = (bf16[2,128,512]{2,1,0:T(8,128)(2,1)S(1)}, bf16[2,128,512]{2,1,0:T(8,128)(2,1)S(1)}, u32[]{:S(2)}, u32[]{:S(2)}) collective-permute-start(bf16[2,128,512]{2,1,0:T(8,128)(2,1)S(1)} %shard_map.59), channel_id=1, source_target_pairs={{0,1},{1,0},{2,3},{3,2},{4,5},{5,4},{6,7},{7,6},{8,9},{9,8},{10,11... | collective-permute-start | bytes 786440 | tf_op jit(solution)/shard_map/ppermute | solution.py:150
  24.3 7.4 %collective-permute-start.1 = (bf16[128,512]{1,0:T(8,128)(2,1)S(1)}, bf16[128,512]{1,0:T(8,128)(2,1)S(1)}, u32[]{:S(2)}, u32[]{:S(2)}) collective-permute-start(bf16[128,512]{1,0:T(8,128)(2,1)S(1)} %get-tuple-element.7), channel_id=1, source_target_pairs={{0,2},{1,3},{2,0},{3,1},{4,6},{5,7},{6,4},{7,5},{8,10},{9,11},{10,... | collective-permute-start | bytes 393224 | tf_op jit(solution)/shard_map/ppermute | solution.py:160
  35.3 25.8 %all-to-all-start.1 = ((bf16[32,16,256]{2,1,0:T(8,128)(2,1)}), bf16[32,16,256]{2,1,0:T(8,128)(2,1)S(1)}, u32[]{:S(2)}, u32[]{:S(2)}) async-start(bf16[32,16,256]{2,1,0:T(8,128)(2,1)} %shard_map.63), calls=%async_computation.1 | async-start | bytes 524288 | tf_op jit(solution)/shard_map/all_to_all | solution.py:176

commit v5 on v3

--- a/solution.py
+++ b/solution.py
@@ -92,7 +92,9 @@
     square_sym = [right_sym[b] + both[b] + both[b].T for b in every]
     total = [2.0 * left_bar[b] - product(split(square_sym[b]), skew_pair[b]) for b in every]
     pieces = [(total[b] - total[b].T).reshape(shares, rows, width) for b in every]
-    out_ref[...] = jnp.concatenate(pieces, axis=1).astype(BF16)
+    sends = jnp.concatenate(pieces, axis=1).astype(BF16)
+    for place in range(shares):
+        out_ref[place] = sends[shares - 1 - place]
 
 
 def acts_kernel(gathered_ref, features_ref, out_ref):
@@ -128,10 +130,16 @@
     blocks, rows, width = skew_param.shape
     scale = 65536.0
     packed = (skew_param * scale).astype(jnp.float16).reshape(1, blocks * rows, width)
+    descending = [list(range(shares - 1, -1, -1))]
     gathered = lax.all_to_all(
-        jnp.broadcast_to(packed, (shares, blocks * rows, width)), "dp", 0, 0, tiled=True
+        jnp.broadcast_to(packed, (shares, blocks * rows, width)),
+        "dp",
+        0,
+        0,
+        axis_index_groups=descending,
+        tiled=True,
     )
-    gathered = (gathered.astype(F32) * (1.0 / scale)).reshape(shares, blocks, rows, width)
+    gathered = (gathered.astype(F32) * (1.0 / scale)).reshape(shares, blocks, rows, width)[::-1]
     own, *sent = kernel_call(
         features_kernel,
         [jax.ShapeDtypeStruct((tokens, own_width), F32)]
@@ -163,7 +171,7 @@
         2 * 18 * blocks * width**3,
         2 << 20,
     )(gathered, grad_rot)
-    arrived = lax.all_to_all(sends, "dp", 0, 0, tiled=True)
+    arrived = lax.all_to_all(sends, "dp", 0, 0, axis_index_groups=descending, tiled=True)
     grad_acts = kernel_call(
         acts_kernel,
         jax.ShapeDtypeStruct((tokens, own_width), BF16),

time: 61.2 us -> 56.8 us (0.928)
  waiting for transfers between devices: 15.9 us -> 9.48 us
  starting transfers between devices: 34 us -> 35.5 us
    all_to_all x1, waiting for transfers between devices: 11.5 us -> 6.15 us  [body(): lax.all_to_all(sends, 'dp', 0, 0, axis_index_groups=descending, tiled=True)]
    all_to_all x1, waiting for transfers between devices: 1.22 us -> 0.01 us  [body(): lax.all_to_all(jnp.broadcast_to(packed, (shares, blocks * rows, width)),...]
    all_to_all x1, starting transfers between devices: 10.3 us -> 11.3 us  [body(): lax.all_to_all(sends, 'dp', 0, 0, axis_index_groups=descending, tiled=True)]
  transfers between devices with their start and end apart: 5 -> 5, of which waited for: 4 -> 3; matrix products, arithmetic and copies ran while one was open for 0% -> 0% of each run, Pallas kernels for 8% -> 9%
where the time goes in v5:
time: 56.8 us; the launch traced here: 55.9 us
  starting transfers between devices  35.5 us (62%)
  waiting for transfers between devices  9.48 us (17%)
  Pallas kernels  7.98 us (14%)
  other arithmetic  1.43 us (3%)
  local copies, waits for them, and re-layouts  0.76 us (1%)
  between operations  0.73 us (1%)
    all_to_all x1, starting transfers between devices, body(): lax.all_to_all(jnp.broadcast_to(packed, (shares, blocks * rows, width)),...  16.6 us
    all_to_all x1, starting transfers between devices, body(): lax.all_to_all(sends, 'dp', 0, 0, axis_index_groups=descending, tiled=True)  11.3 us
    ppermute x3, starting transfers between devices, body(): lax.ppermute(sent[turn - 1], 'outcol', [(i, i ^ turn) for i in range(part...  7.59 us
    all_to_all x1, waiting for transfers between devices, body(): lax.all_to_all(sends, 'dp', 0, 0, axis_index_groups=descending, tiled=True)  6.15 us
    ppermute x3, waiting for transfers between devices, body(): lax.ppermute(sent[turn - 1], 'outcol', [(i, i ^ turn) for i in range(part...  3.33 us
    pallas_call x1, Pallas kernels, body(): kernel_call(acts_kernel, jax.ShapeDtypeStruct((tokens, own_width), BF16),...  2.9 us
    pallas_call x1, Pallas kernels, body(): kernel_call(chain_kernel, jax.ShapeDtypeStruct((shares, blocks * rows, wi...  2.89 us
    pallas_call x1, Pallas kernels, body(): kernel_call(features_kernel, [jax.ShapeDtypeStruct((tokens, own_width), F...  1.93 us
  transfers between devices with their start and end apart: 5, of which 3 were waited for; matrix products, arithmetic and copies ran while one was open for 0% of the time, Pallas kernels for 9%

profile of v5, /device:TPU:6, one launch (start us, length us, event | category | flops | bytes accessed | tf_op | source)
XLA Modules:
  0.0 55.9 jit_solution(7296252641593885956)
XLA Ops:
  0.6 0.7 %fusion = f16[16,256]{1,0:T(8,128)(2,1)S(1)} fusion(f32[2,8,256]{2,1,0:T(8,128)} %param.7), kind=kLoop, calls=%fused_computation.3 | loop fusion | flops 8192 | bytes 24576 | tf_op jit(solution)/shard_map/broadcast_in_dim | solution.py:135
  1.4 0.7 %broadcast_in_dim.8 = f16[32,16,256]{2,1,0:T(8,128)(2,1)} broadcast(f16[16,256]{1,0:T(8,128)(2,1)S(1)} %fusion), dimensions={1,2} | broadcast | bytes 270336 | tf_op jit(solution)/shard_map/broadcast_in_dim | solution.py:135
  2.1 0.0 copy-start.1
  2.1 16.6 %all-to-all-start = ((f16[32,16,256]{2,1,0:T(8,128)(2,1)}), f16[32,16,256]{2,1,0:T(8,128)(2,1)S(1)}, u32[]{:S(2)}, u32[]{:S(2)}) async-start(f16[32,16,256]{2,1,0:T(8,128)(2,1)} %broadcast_in_dim.8), calls=%async_computation | async-start | bytes 524288 | tf_op jit(solution)/shard_map/all_to_all | solution.py:134
  18.7 0.0 copy-done.1
  18.7 0.0 copy-start
  18.7 1.9 %shard_map.59 = (f32[128,512]{1,0:T(8,128)S(1)}, bf16[128,512]{1,0:T(8,128)(2,1)S(1)}, bf16[128,512]{1,0:T(8,128)(2,1)S(1)}, bf16[128,512]{1,0:T(8,128)(2,1)S(1)}) custom-call(bf16[128,256]{1,0:T(8,128)(2,1)S(1)} %copy-done.1, bf16[2048,256]{1,0:T(8,128)(2,1)} %weight_ref.1), custom_call_target="tpu_custom_call" | custom-call | flops 134217728 | bytes 2097152 | tf_op jit(solution)/shard_map/pallas_call | solution.py:143
  20.6 2.1 %collective-permute-start = (bf16[128,512]{1,0:T(8,128)(2,1)S(1)}, bf16[128,512]{1,0:T(8,128)(2,1)S(1)}, u32[]{:S(2)}, u32[]{:S(2)}) collective-permute-start(bf16[128,512]{1,0:T(8,128)(2,1)S(1)} %get-tuple-element.9), channel_id=1, source_target_pairs={{0,3},{1,2},{2,1},{3,0},{4,7},{5,6},{6,5},{7,4},{8,11},{9,10},{10,... | collective-permute-start | bytes 393224 | tf_op jit(solution)/shard_map/ppermute | solution.py:156
  22.7 3.0 %collective-permute-start.1 = (bf16[128,512]{1,0:T(8,128)(2,1)S(1)}, bf16[128,512]{1,0:T(8,128)(2,1)S(1)}, u32[]{:S(2)}, u32[]{:S(2)}) collective-permute-start(bf16[128,512]{1,0:T(8,128)(2,1)S(1)} %get-tuple-element.10), channel_id=1, source_target_pairs={{0,2},{1,3},{2,0},{3,1},{4,6},{5,7},{6,4},{7,5},{8,10},{9,11},{10,... | collective-permute-start | bytes 393224 | tf_op jit(solution)/shard_map/ppermute | solution.py:156
  25.8 2.5 %collective-permute-start.2 = (bf16[128,512]{1,0:T(8,128)(2,1)S(1)}, bf16[128,512]{1,0:T(8,128)(2,1)S(1)}, u32[]{:S(2)}, u32[]{:S(2)}) collective-permute-start(bf16[128,512]{1,0:T(8,128)(2,1)S(1)} %get-tuple-element.11), channel_id=1, source_target_pairs={{0,1},{1,0},{2,3},{3,2},{4,5},{5,4},{6,7},{7,6},{8,9},{9,8},{10,11... | collective-permute-start | bytes 393224 | tf_op jit(solution)/shard_map/ppermute | solution.py:156
  28.2 0.8 %collective-permute-done.refs_0_ = bf16[128,512]{1,0:T(8,128)(2,1)S(1)} collective-permute-done((bf16[128,512]{1,0:T(8,128)(2,1)S(1)}, bf16[128,512]{1,0:T(8,128)(2,1)S(1)}, u32[]{:S(2)}, u32[]{:S(2)}) %collective-permute-start) | collective-permute-done | bytes 131104 | tf_op jit(solution)/shard_map/ppermute | solution.py:156
  29.1 2.5 %collective-permute-done.1.refs_1_ = bf16[128,512]{1,0:T(8,128)(2,1)S(1)} collective-permute-done((bf16[128,512]{1,0:T(8,128)(2,1)S(1)}, bf16[128,512]{1,0:T(8,128)(2,1)S(1)}, u32[]{:S(2)}, u32[]{:S(2)}) %collective-permute-start.1) | collective-permute-done | bytes 131104 | tf_op jit(solution)/shard_map/ppermute | solution.py:156
  31.6 0.0 collective-permute-done.2.refs_2_
  31.6 0.0 copy-done
  31.6 0.3 shard_map.60
  31.8 0.0 all-to-all-done
  31.9 0.1 multiply_bitcast_fusion
  32.0 2.9 %shard_map.62 = bf16[32,16,256]{2,1,0:T(8,128)(2,1)} custom-call(f32[32,2,8,256]{3,2,1,0:T(8,128)S(1)} %rev.3.gathered_ref, f32[2,256,256]{2,1,0:T(8,128)S(1)} %get-tuple-element.13.grad_ref), custom_call_target="tpu_custom_call" | custom-call | flops 1207959552 | bytes 2097152 | tf_op jit(solution)/shard_map/pallas_call | solution.py:168
  34.8 11.3 %all-to-all-start.1 = ((bf16[32,16,256]{2,1,0:T(8,128)(2,1)}), bf16[32,16,256]{2,1,0:T(8,128)(2,1)S(1)}, u32[]{:S(2)}, u32[]{:S(2)}) async-start(bf16[32,16,256]{2,1,0:T(8,128)(2,1)} %shard_map.62), calls=%async_computation.1 | async-start | bytes 524288 | tf_op jit(solution)/shard_map/all_to_all | solution.py:174
  46.2 2.9 %shard_map.61 = bf16[128,512]{1,0:T(8,128)(2,1)} custom-call(f32[32,2,8,256]{3,2,1,0:T(8,128)S(1)} %rev.3.gathered_ref, bf16[128,512]{1,0:T(8,128)(2,1)S(1)} %get-tuple-element.12.features_ref), custom_call_target="tpu_custom_call" | custom-call | flops 671088640 | bytes 1048576 | tf_op jit(solution)/shard_map/pallas_call | solution.py:175
  49.1 6.2 %all-to-all-done.1 = bf16[32,16,256]{2,1,0:T(8,128)(2,1)S(1)} async-done(((bf16[32,16,256]{2,1,0:T(8,128)(2,1)}), bf16[32,16,256]{2,1,0:T(8,128)(2,1)S(1)}, u32[]{:S(2)}, u32[]{:S(2)}) %all-to-all-start.1) | async-done | bytes 262176 | tf_op jit(solution)/shard_map/all_to_all | solution.py:174
  55.2 0.7 %convert_reduce_fusion = f32[16,256]{1,0:T(8,128)} fusion(bf16[32,16,256]{2,1,0:T(8,128)(2,1)S(1)} %all-to-all-done.1), kind=kLoop, calls=%fused_computation | loop fusion | flops 258048 | bytes 278528 | tf_op jit(solution)/shard_map/reduce_sum | solution.py:181
  (1 shorter events, 0.0 us)
Async XLA Ops:
  2.1 16.6 %copy-start.1 = (bf16[128,256]{1,0:T(8,128)(2,1)S(1)}, bf16[128,256]{1,0:T(8,128)(2,1)}, u32[]{:S(2)}) copy-start(bf16[128,256]{1,0:T(8,128)(2,1)} %cotangent_ref.1) | copy-start | bytes 196612
  2.1 29.8 %all-to-all-start = ((f16[32,16,256]{2,1,0:T(8,128)(2,1)}), f16[32,16,256]{2,1,0:T(8,128)(2,1)S(1)}, u32[]{:S(2)}, u32[]{:S(2)}) async-start(f16[32,16,256]{2,1,0:T(8,128)(2,1)} %broadcast_in_dim.8), calls=%async_computation | async-start | bytes 524288 | tf_op jit(solution)/shard_map/all_to_all | solution.py:134
  18.7 12.9 %copy-start = (bf16[128,512]{1,0:T(8,128)(2,1)S(1)}, bf16[128,512]{1,0:T(8,128)(2,1)}, u32[]{:S(2)}) copy-start(bf16[128,512]{1,0:T(8,128)(2,1)} %acts_ref.1) | copy-start | bytes 393220
  20.6 8.4 %collective-permute-start = (bf16[128,512]{1,0:T(8,128)(2,1)S(1)}, bf16[128,512]{1,0:T(8,128)(2,1)S(1)}, u32[]{:S(2)}, u32[]{:S(2)}) collective-permute-start(bf16[128,512]{1,0:T(8,128)(2,1)S(1)} %get-tuple-element.9), channel_id=1, source_target_pairs={{0,3},{1,2},{2,1},{3,0},{4,7},{5,6},{6,5},{7,4},{8,11},{9,10},{10,... | collective-permute-start | bytes 393224 | tf_op jit(solution)/shard_map/ppermute | solution.py:156
  22.7 8.9 %collective-permute-start.1 = (bf16[128,512]{1,0:T(8,128)(2,1)S(1)}, bf16[128,512]{1,0:T(8,128)(2,1)S(1)}, u32[]{:S(2)}, u32[]{:S(2)}) collective-permute-start(bf16[128,512]{1,0:T(8,128)(2,1)S(1)} %get-tuple-element.10), channel_id=1, source_target_pairs={{0,2},{1,3},{2,0},{3,1},{4,6},{5,7},{6,4},{7,5},{8,10},{9,11},{10,... | collective-permute-start | bytes 393224 | tf_op jit(solution)/shard_map/ppermute | solution.py:156
  25.8 5.8 %collective-permute-start.2 = (bf16[128,512]{1,0:T(8,128)(2,1)S(1)}, bf16[128,512]{1,0:T(8,128)(2,1)S(1)}, u32[]{:S(2)}, u32[]{:S(2)}) collective-permute-start(bf16[128,512]{1,0:T(8,128)(2,1)S(1)} %get-tuple-element.11), channel_id=1, source_target_pairs={{0,1},{1,0},{2,3},{3,2},{4,5},{5,4},{6,7},{7,6},{8,9},{9,8},{10,11... | collective-permute-start | bytes 393224 | tf_op jit(solution)/shard_map/ppermute | solution.py:156
  34.8 20.4 %all-to-all-start.1 = ((bf16[32,16,256]{2,1,0:T(8,128)(2,1)}), bf16[32,16,256]{2,1,0:T(8,128)(2,1)S(1)}, u32[]{:S(2)}, u32[]{:S(2)}) async-start(bf16[32,16,256]{2,1,0:T(8,128)(2,1)} %shard_map.62), calls=%async_computation.1 | async-start | bytes 524288 | tf_op jit(solution)/shard_map/all_to_all | solution.py:174

commit v6 on v5

v6 whole, which is shorter than its diff:
```python
import jax
import jax.numpy as jnp
from jax import lax
from jax.experimental import pallas as pl
from jax.experimental.pallas import tpu as pltpu
from jax.sharding import PartitionSpec as P

BF16 = jnp.bfloat16
F32 = jnp.float32


def split(x):
    high = x.astype(BF16)
    return high, (x - high.astype(F32)).astype(BF16)


def product(left, right):
    dot = lambda a, b: jnp.dot(a, b, preferred_element_type=F32)
    return dot(left[0], right[0]) + (dot(left[0], right[1]) + dot(left[1], right[0]))


def factors(gathered, block):
    shares = gathered.shape[0]
    param = jnp.concatenate(
        [gathered[shares - 1 - share, block] for share in range(shares)], axis=0
    )
    skew = param - param.T
    skew_pair = split(skew)
    square = product(skew_pair, skew_pair)
    square_pair = split(square)
    fourth = product(square_pair, square_pair)
    return skew, skew_pair, square, square_pair, square + fourth


def partial_sum(cotangent_ref, weight):
    return lax.dot_general(
        cotangent_ref[...], weight, (((1,), (1,)), ((), ())), preferred_element_type=F32
    )


def far_kernel(cotangent_ref, weight_ref, *refs):
    out_refs, held, semaphores = refs[:-2], refs[-2], refs[-1]
    width = held.shape[1]
    me = lax.axis_index("outcol")
    copies = []
    for place in range(len(out_refs)):
        first = pl.multiple_of((me ^ (3 - place)) * width, width)
        copies.append(
            pltpu.make_async_copy(
                weight_ref.at[pl.ds(first, width), :], held.at[place], semaphores.at[place]
            )
        )
        copies[place].start()
    for place, out_ref in enumerate(out_refs):
        copies[place].wait()
        out_ref[...] = partial_sum(cotangent_ref, held[place]).astype(BF16)


def near_kernel(cotangent_ref, weight_ref, sent_ref, own_ref):
    width = own_ref.shape[1]
    me = lax.axis_index("outcol")
    for turn, out_ref in ((1, sent_ref), (0, own_ref)):
        first = pl.multiple_of((me ^ turn) * width, width)
        part = partial_sum(cotangent_ref, weight_ref[pl.ds(first, width), :])
        out_ref[...] = part.astype(out_ref.dtype)


def powers_kernel(gathered_ref, *out_refs):
    shares, blocks, rows, width = gathered_ref.shape
    every = range(blocks)
    param = [
        jnp.concatenate([gathered_ref[shares - 1 - share, b] for share in range(shares)], axis=0)
        for b in every
    ]
    skew = [param[b] - param[b].T for b in every]
    skew_pair = [split(skew[b]) for b in every]
    square = [product(skew_pair[b], skew_pair[b]) for b in every]
    square_pair = [split(square[b]) for b in every]
    left_pair = [split(square[b] - 2.0 * skew[b]) for b in every]
    fourth = [product(square_pair[b], square_pair[b]) for b in every]
    rest_pair = [split(square[b] + fourth[b]) for b in every]
    for place, pair in enumerate((skew_pair, square_pair, left_pair, rest_pair)):
        for b in every:
            out_refs[2 * place][b] = pair[b][0]
            out_refs[2 * place + 1][b] = pair[b][1]


def chain_kernel(*refs):
    power_refs, (acts_ref, own_ref), part_refs = refs[:8], refs[8:10], refs[10:-2]
    features_ref, out_ref = refs[-2:]
    blocks, width, _ = power_refs[0].shape
    every = range(blocks)
    skew, square, left, rest = [
        [(power_refs[2 * place][b], power_refs[2 * place + 1][b]) for b in every]
        for place in range(4)
    ]
    features = own_ref[...]
    for part_ref in part_refs:
        features = features + part_ref[...].astype(F32)
    features = features.astype(BF16)
    features_ref[...] = features
    acts = acts_ref[...]
    cols = [slice(b * width, (b + 1) * width) for b in every]
    grad = [
        lax.dot_general(
            acts[:, cols[b]],
            features[:, cols[b]],
            (((0,), (0,)), ((), ())),
            preferred_element_type=F32,
        )
        for b in every
    ]
    grad_pair = [split(grad[b]) for b in every]
    right_bar = [grad[b] + product(left[b], grad_pair[b]) for b in every]
    left_bar = [grad[b] + product(grad_pair[b], rest[b]) for b in every]
    right_sym = [right_bar[b] + right_bar[b].T for b in every]
    both = [left_bar[b] + product(split(right_sym[b]), square[b]) for b in every]
    square_sym = [right_sym[b] + both[b] + both[b].T for b in every]
    total = [2.0 * left_bar[b] - product(split(square_sym[b]), skew[b]) for b in every]
    shares = out_ref.shape[0]
    pieces = [(total[b] - total[b].T).reshape(shares, -1, width) for b in every]
    sends = jnp.concatenate(pieces, axis=1).astype(BF16)
    for place in range(shares):
        out_ref[place] = sends[shares - 1 - place]


def acts_kernel(gathered_ref, features_ref, out_ref):
    blocks, width = gathered_ref.shape[1], gathered_ref.shape[-1]
    for block in range(blocks):
        skew, _, square, _, rest = factors(gathered_ref, block)
        first = 2.0 * skew + square
        row = lax.broadcasted_iota(jnp.int32, (width, width), 0)
        col = lax.broadcasted_iota(jnp.int32, (width, width), 1)
        identity = jnp.where(row == col, 1.0, 0.0).astype(F32)
        rotation = (identity + first + rest + product(split(first), split(rest))).astype(BF16)
        cols = slice(block * width, (block + 1) * width)
        out_ref[:, cols] = lax.dot_general(
            features_ref[:, cols], rotation, (((1,), (1,)), ((), ())), preferred_element_type=F32
        ).astype(BF16)


def kernel_call(kernel, out_shape, flops, moved, **specs):
    return pl.pallas_call(
        kernel,
        out_shape=out_shape,
        compiler_params=pltpu.CompilerParams(vmem_limit_bytes=24 << 20),
        cost_estimate=pl.CostEstimate(flops=flops, bytes_accessed=moved, transcendentals=0),
        **specs,
    )


def body(activations, cotangent, base_weight, skew_param):
    shares = lax.axis_size("dp")
    parts = lax.axis_size("outcol")
    tokens, own_width = activations.shape
    depth = cotangent.shape[1]
    blocks, rows, width = skew_param.shape
    scale = 65536.0
    packed = (skew_param * scale).astype(jnp.float16).reshape(1, blocks * rows, width)
    descending = [list(range(shares - 1, -1, -1))]
    gathered = lax.all_to_all(
        jnp.broadcast_to(packed, (shares, blocks * rows, width)),
        "dp",
        0,
        0,
        axis_index_groups=descending,
        tiled=True,
    )
    gathered = (gathered.astype(F32) * (1.0 / scale)).reshape(shares, blocks, rows, width)
    work = tokens * depth * own_width * parts
    far = kernel_call(
        far_kernel,
        [jax.ShapeDtypeStruct((tokens, own_width), BF16)] * 2,
        work,
        1 << 20,
        in_specs=[pl.BlockSpec(memory_space=pltpu.VMEM), pl.BlockSpec(memory_space=pltpu.HBM)],
        scratch_shapes=[
            pltpu.VMEM((2, own_width, depth), BF16),
            pltpu.SemaphoreType.DMA((2,)),
        ],
    )(cotangent, pltpu.with_memory_space_constraint(base_weight, pltpu.HBM))
    near, own = kernel_call(
        near_kernel,
        (
            jax.ShapeDtypeStruct((tokens, own_width), BF16),
            jax.ShapeDtypeStruct((tokens, own_width), F32),
        ),
        work,
        1 << 20,
    )(cotangent, base_weight)
    received = [
        lax.ppermute(part, "outcol", [(i, i ^ turn) for i in range(parts)])
        for turn, part in ((3, far[0]), (2, far[1]), (1, near))
    ]
    powers = kernel_call(
        powers_kernel,
        [jax.ShapeDtypeStruct((blocks, width, width), BF16)] * 8,
        2 * 6 * blocks * width**3,
        2 << 20,
    )(gathered)
    features, sends = kernel_call(
        chain_kernel,
        (
            jax.ShapeDtypeStruct((tokens, own_width), BF16),
            jax.ShapeDtypeStruct((shares, blocks * rows, width), BF16),
        ),
        2 * 12 * blocks * width**3,
        2 << 20,
    )(*powers, activations, own, *received)
    arrived = lax.all_to_all(sends, "dp", 0, 0, axis_index_groups=descending, tiled=True)
    grad_acts = kernel_call(
        acts_kernel,
        jax.ShapeDtypeStruct((tokens, own_width), BF16),
        2 * 10 * blocks * width**3,
        1 << 20,
    )(gathered, features)
    grad_skew = jnp.sum(arrived.astype(F32), axis=0).reshape(blocks, rows, width)
    return grad_acts, grad_skew


def solution(mesh):
    return jax.shard_map(
        body,
        mesh=mesh,
        in_specs=(
            P("dp", ("inblk", "outcol")),
            P("dp", "outcol"),
            P("inblk", "outcol"),
            P(("inblk", "outcol"), "dp", None),
        ),
        out_specs=(P("dp", ("inblk", "outcol")), P(("inblk", "outcol"), "dp", None)),
        check_vma=False,
    )
```

time: 56.8 us -> 56.1 us (0.988)
  waiting for transfers between devices: 9.48 us -> 8.14 us
  local copies, waits for them, and re-layouts: 0.76 us -> 1.58 us
    ppermute x3, waiting for transfers between devices: 3.33 us -> 1.96 us  [body(): lax.ppermute(part, 'outcol', [(i, i ^ turn) for i in range(parts)])]
    unnamed x4 -> x6, local copies, waits for them, and re-layouts: 0.01 us -> 0.85 us
    pallas_call x3 -> x4, Pallas kernels: 5.08 us -> 5 us  [the longest x1 2.3 us: body(): kernel_call(chain_kernel, (jax.ShapeDtypeStruct((tokens, own_width), BF16...]
  transfers between devices with their start and end apart: 5 -> 5, of which waited for: 3 -> 2; matrix products, arithmetic and copies ran while one was open for 0% -> 0% of each run, Pallas kernels for 9% -> 10%
where the time goes in v6:
time: 56.1 us; the launch traced here: 55.2 us
  starting transfers between devices  35.3 us (63%)
  waiting for transfers between devices  8.14 us (15%)
  Pallas kernels  7.91 us (14%)
  local copies, waits for them, and re-layouts  1.58 us (3%)
  other arithmetic  1.52 us (3%)
  between operations  0.75 us (1%)
    all_to_all x1, starting transfers between devices, body(): lax.all_to_all(jnp.broadcast_to(packed, (shares, blocks * rows, width)),...  16.5 us
    all_to_all x1, starting transfers between devices, body(): lax.all_to_all(sends, 'dp', 0, 0, axis_index_groups=descending, tiled=True)  11.3 us
    ppermute x3, starting transfers between devices, body(): lax.ppermute(part, 'outcol', [(i, i ^ turn) for i in range(parts)])  7.58 us
    all_to_all x1, waiting for transfers between devices, body(): lax.all_to_all(sends, 'dp', 0, 0, axis_index_groups=descending, tiled=True)  6.18 us
    pallas_call x1, Pallas kernels, body(): kernel_call(acts_kernel, jax.ShapeDtypeStruct((tokens, own_width), BF16),...  2.9 us
    pallas_call x1, Pallas kernels, body(): kernel_call(chain_kernel, (jax.ShapeDtypeStruct((tokens, own_width), BF16...  2.3 us
    ppermute x3, waiting for transfers between devices, body(): lax.ppermute(part, 'outcol', [(i, i ^ turn) for i in range(parts)])  1.96 us
    pallas_call x1, Pallas kernels, body(): kernel_call(far_kernel, [jax.ShapeDtypeStruct((tokens, own_width), BF16)]...  1.42 us
  transfers between devices with their start and end apart: 5, of which 2 were waited for; matrix products, arithmetic and copies ran while one was open for 0% of the time, Pallas kernels for 10%

profile of v6, /device:TPU:6, one launch (start us, length us, event | category | flops | bytes accessed | tf_op | source)
XLA Modules:
  0.0 55.2 jit_solution(9368822557324410563)
XLA Ops:
  0.6 0.0 copy-start
  0.6 0.8 %fusion = f16[16,256]{1,0:T(8,128)(2,1)S(1)} fusion(f32[2,8,256]{2,1,0:T(8,128)} %param.7), kind=kLoop, calls=%fused_computation.3 | loop fusion | flops 8192 | bytes 24576 | tf_op jit(solution)/shard_map/broadcast_in_dim | solution.py:162
  1.5 0.7 %broadcast_in_dim.8 = f16[32,16,256]{2,1,0:T(8,128)(2,1)} broadcast(f16[16,256]{1,0:T(8,128)(2,1)S(1)} %fusion), dimensions={1,2} | broadcast | bytes 270336 | tf_op jit(solution)/shard_map/broadcast_in_dim | solution.py:162
  2.2 16.5 %all-to-all-start = ((f16[32,16,256]{2,1,0:T(8,128)(2,1)}), f16[32,16,256]{2,1,0:T(8,128)(2,1)S(1)}, u32[]{:S(2)}, u32[]{:S(2)}) async-start(f16[32,16,256]{2,1,0:T(8,128)(2,1)} %broadcast_in_dim.8), calls=%async_computation | async-start | bytes 524288 | tf_op jit(solution)/shard_map/all_to_all | solution.py:161
  18.6 0.0 copy-start.1
  18.7 0.8 %copy-done.1 = bf16[128,256]{1,0:T(8,128)(2,1)S(1)} copy-done((bf16[128,256]{1,0:T(8,128)(2,1)S(1)}, bf16[128,256]{1,0:T(8,128)(2,1)}, u32[]{:S(2)}) %copy-start.1) | copy-done | bytes 65560
  19.5 1.4 %shard_map.61 = (bf16[128,512]{1,0:T(8,128)(2,1)S(1)}, bf16[128,512]{1,0:T(8,128)(2,1)S(1)}) custom-call(bf16[128,256]{1,0:T(8,128)(2,1)S(1)} %copy-done.1, bf16[2048,256]{1,0:T(8,128)(2,1)} %weight_ref.3), custom_call_target="tpu_custom_call" | custom-call | flops 67108864 | bytes 1048576 | tf_op jit(solution)/shard_map/pallas_call | solution.py:171
  20.9 2.1 %collective-permute-start = (bf16[128,512]{1,0:T(8,128)(2,1)S(1)}, bf16[128,512]{1,0:T(8,128)(2,1)S(1)}, u32[]{:S(2)}, u32[]{:S(2)}) collective-permute-start(bf16[128,512]{1,0:T(8,128)(2,1)S(1)} %get-tuple-element.25), channel_id=1, source_target_pairs={{0,3},{1,2},{2,1},{3,0},{4,7},{5,6},{6,5},{7,4},{8,11},{9,10},{10,... | collective-permute-start | bytes 393224 | tf_op jit(solution)/shard_map/ppermute | solution.py:192
  23.0 3.0 %collective-permute-start.1 = (bf16[128,512]{1,0:T(8,128)(2,1)S(1)}, bf16[128,512]{1,0:T(8,128)(2,1)S(1)}, u32[]{:S(2)}, u32[]{:S(2)}) collective-permute-start(bf16[128,512]{1,0:T(8,128)(2,1)S(1)} %get-tuple-element.26), channel_id=1, source_target_pairs={{0,2},{1,3},{2,0},{3,1},{4,6},{5,7},{6,4},{7,5},{8,10},{9,11},{10,... | collective-permute-start | bytes 393224 | tf_op jit(solution)/shard_map/ppermute | solution.py:192
  26.0 0.0 copy-done
  26.0 0.3 shard_map.60
  26.4 2.5 %collective-permute-start.2 = (bf16[128,512]{1,0:T(8,128)(2,1)S(1)}, bf16[128,512]{1,0:T(8,128)(2,1)S(1)}, u32[]{:S(2)}, u32[]{:S(2)}) collective-permute-start(bf16[128,512]{1,0:T(8,128)(2,1)S(1)} %get-tuple-element.27), channel_id=1, source_target_pairs={{0,1},{1,0},{2,3},{3,2},{4,5},{5,4},{6,7},{7,6},{8,9},{9,8},{10,11... | collective-permute-start | bytes 393224 | tf_op jit(solution)/shard_map/ppermute | solution.py:192
  28.8 0.0 all-to-all-done
  28.9 0.1 multiply_bitcast_fusion.gathered_ref
  28.9 0.0 copy-start.2
  28.9 1.0 %shard_map.59 = (bf16[2,256,256]{2,1,0:T(8,128)(2,1)S(1)}, bf16[2,256,256]{2,1,0:T(8,128)(2,1)S(1)}, bf16[2,256,256]{2,1,0:T(8,128)(2,1)S(1)}, bf16[2,256,256]{2...) custom-call(f32[32,2,8,256]{3,2,1,0:T(8,128)S(1)} %multiply_bitcast_, ...), custom_call_target="tpu_custom_call" | custom-call | flops 402653184 | bytes 2097152 | tf_op jit(solution)/shard_map/pallas_call | solution.py:195
  29.9 0.0 collective-permute-done.refs_10_
  29.9 2.0 %collective-permute-done.1.refs_11_ = bf16[128,512]{1,0:T(8,128)(2,1)S(1)} collective-permute-done((bf16[128,512]{1,0:T(8,128)(2,1)S(1)}, bf16[128,512]{1,0:T(8,128)(2,1)S(1)}, u32[]{:S(2)}, u32[]{:S(2)}) %collective-permute-start.1) | collective-permute-done | bytes 131104 | tf_op jit(solution)/shard_map/ppermute | solution.py:192
  31.9 0.0 collective-permute-done.2.refs_12_
  31.9 0.0 copy-done.2
  31.9 2.3 %shard_map.62 = (bf16[128,512]{1,0:T(8,128)(2,1)S(1)}, bf16[32,16,256]{2,1,0:T(8,128)(2,1)}) custom-call(bf16[2,256,256]{2,1,0:T(8,128)(2,1)S(1)} %get-tuple-element.16.refs_0_, bf16[2,256,256]{2,1,0:T(8,128)(2,1)S(1)} %get-tuple-element.17.refs_1_, bf16[2,256,256]{2,1,0:T(8,128)(2,1)S(1)} %get-tuple-element.18.refs_2_, ...), custom_call_target="tpu_custom_call" | custom-call | flops 805306368 | bytes 2097152 | tf_op jit(solution)/shard_map/pallas_call | solution.py:201
  34.2 11.3 %all-to-all-start.1 = ((bf16[32,16,256]{2,1,0:T(8,128)(2,1)}), bf16[32,16,256]{2,1,0:T(8,128)(2,1)S(1)}, u32[]{:S(2)}, u32[]{:S(2)}) async-start(bf16[32,16,256]{2,1,0:T(8,128)(2,1)} %get-tuple-element.29), calls=%async_computation.1 | async-start | bytes 524288 | tf_op jit(solution)/shard_map/all_to_all | solution.py:210
  45.5 2.9 %shard_map.63 = bf16[128,512]{1,0:T(8,128)(2,1)} custom-call(f32[32,2,8,256]{3,2,1,0:T(8,128)S(1)} %multiply_bitcast_fusion.gathered_ref, bf16[128,512]{1,0:T(8,128)(2,1)S(1)} %get-tuple-element.28.features_ref), custom_call_target="tpu_custom_call" | custom-call | flops 671088640 | bytes 1048576 | tf_op jit(solution)/shard_map/pallas_call | solution.py:211
  48.4 6.2 %all-to-all-done.1 = bf16[32,16,256]{2,1,0:T(8,128)(2,1)S(1)} async-done(((bf16[32,16,256]{2,1,0:T(8,128)(2,1)}), bf16[32,16,256]{2,1,0:T(8,128)(2,1)S(1)}, u32[]{:S(2)}, u32[]{:S(2)}) %all-to-all-start.1) | async-done | bytes 262176 | tf_op jit(solution)/shard_map/all_to_all | solution.py:210
  54.6 0.7 %convert_reduce_fusion = f32[16,256]{1,0:T(8,128)} fusion(bf16[32,16,256]{2,1,0:T(8,128)(2,1)S(1)} %all-to-all-done.1), kind=kLoop, calls=%fused_computation | loop fusion | flops 258048 | bytes 278528 | tf_op jit(solution)/shard_map/reduce_sum | solution.py:217
Async XLA Ops:
  0.6 25.4 %copy-start = (bf16[2048,256]{1,0:T(8,128)(2,1)S(1)}, bf16[2048,256]{1,0:T(8,128)(2,1)}, u32[]{:S(2)}) copy-start(bf16[2048,256]{1,0:T(8,128)(2,1)} %weight_ref.3) | copy-start | bytes 3145732
  2.2 26.7 %all-to-all-start = ((f16[32,16,256]{2,1,0:T(8,128)(2,1)}), f16[32,16,256]{2,1,0:T(8,128)(2,1)S(1)}, u32[]{:S(2)}, u32[]{:S(2)}) async-start(f16[32,16,256]{2,1,0:T(8,128)(2,1)} %broadcast_in_dim.8), calls=%async_computation | async-start | bytes 524288 | tf_op jit(solution)/shard_map/all_to_all | solution.py:161
  18.6 0.8 %copy-start.1 = (bf16[128,256]{1,0:T(8,128)(2,1)S(1)}, bf16[128,256]{1,0:T(8,128)(2,1)}, u32[]{:S(2)}) copy-start(bf16[128,256]{1,0:T(8,128)(2,1)} %cotangent_ref.3) | copy-start | bytes 196612
  20.9 9.0 %collective-permute-start = (bf16[128,512]{1,0:T(8,128)(2,1)S(1)}, bf16[128,512]{1,0:T(8,128)(2,1)S(1)}, u32[]{:S(2)}, u32[]{:S(2)}) collective-permute-start(bf16[128,512]{1,0:T(8,128)(2,1)S(1)} %get-tuple-element.25), channel_id=1, source_target_pairs={{0,3},{1,2},{2,1},{3,0},{4,7},{5,6},{6,5},{7,4},{8,11},{9,10},{10,... | collective-permute-start | bytes 393224 | tf_op jit(solution)/shard_map/ppermute | solution.py:192
  23.0 8.9 %collective-permute-start.1 = (bf16[128,512]{1,0:T(8,128)(2,1)S(1)}, bf16[128,512]{1,0:T(8,128)(2,1)S(1)}, u32[]{:S(2)}, u32[]{:S(2)}) collective-permute-start(bf16[128,512]{1,0:T(8,128)(2,1)S(1)} %get-tuple-element.26), channel_id=1, source_target_pairs={{0,2},{1,3},{2,0},{3,1},{4,6},{5,7},{6,4},{7,5},{8,10},{9,11},{10,... | collective-permute-start | bytes 393224 | tf_op jit(solution)/shard_map/ppermute | solution.py:192
  26.4 5.5 %collective-permute-start.2 = (bf16[128,512]{1,0:T(8,128)(2,1)S(1)}, bf16[128,512]{1,0:T(8,128)(2,1)S(1)}, u32[]{:S(2)}, u32[]{:S(2)}) collective-permute-start(bf16[128,512]{1,0:T(8,128)(2,1)S(1)} %get-tuple-element.27), channel_id=1, source_target_pairs={{0,1},{1,0},{2,3},{3,2},{4,5},{5,4},{6,7},{7,6},{8,9},{9,8},{10,11... | collective-permute-start | bytes 393224 | tf_op jit(solution)/shard_map/ppermute | solution.py:192
  28.9 3.0 %copy-start.2 = (bf16[128,512]{1,0:T(8,128)(2,1)S(1)}, bf16[128,512]{1,0:T(8,128)(2,1)}, u32[]{:S(2)}) copy-start(bf16[128,512]{1,0:T(8,128)(2,1)} %refs_8_.1) | copy-start | bytes 393220
  34.2 20.4 %all-to-all-start.1 = ((bf16[32,16,256]{2,1,0:T(8,128)(2,1)}), bf16[32,16,256]{2,1,0:T(8,128)(2,1)S(1)}, u32[]{:S(2)}, u32[]{:S(2)}) async-start(bf16[32,16,256]{2,1,0:T(8,128)(2,1)} %get-tuple-element.29), calls=%async_computation.1 | async-start | bytes 524288 | tf_op jit(solution)/shard_map/all_to_all | solution.py:210

commit v7 on v6

--- a/solution.py
+++ b/solution.py
@@ -38,28 +38,24 @@
     )
 
 
-def far_kernel(cotangent_ref, weight_ref, *refs):
-    out_refs, held, semaphores = refs[:-2], refs[-2], refs[-1]
-    width = held.shape[1]
+def far_kernel(cotangent_ref, weight_ref, out_ref, cotangent, weight, semaphores):
+    width = out_ref.shape[1]
+    first = pl.multiple_of((lax.axis_index("outcol") ^ 3) * width, width)
+    copies = [
+        pltpu.make_async_copy(weight_ref.at[pl.ds(first, width), :], weight, semaphores.at[0]),
+        pltpu.make_async_copy(cotangent_ref, cotangent, semaphores.at[1]),
+    ]
+    for copy in copies:
+        copy.start()
+    for copy in copies:
+        copy.wait()
+    out_ref[...] = partial_sum(cotangent, weight[...]).astype(BF16)
+
+
+def near_kernel(cotangent_ref, weight_ref, *out_refs):
+    width = out_refs[0].shape[1]
     me = lax.axis_index("outcol")
-    copies = []
-    for place in range(len(out_refs)):
-        first = pl.multiple_of((me ^ (3 - place)) * width, width)
-        copies.append(
-            pltpu.make_async_copy(
-                weight_ref.at[pl.ds(first, width), :], held.at[place], semaphores.at[place]
-            )
-        )
-        copies[place].start()
-    for place, out_ref in enumerate(out_refs):
-        copies[place].wait()
-        out_ref[...] = partial_sum(cotangent_ref, held[place]).astype(BF16)
-
-
-def near_kernel(cotangent_ref, weight_ref, sent_ref, own_ref):
-    width = own_ref.shape[1]
-    me = lax.axis_index("outcol")
-    for turn, out_ref in ((1, sent_ref), (0, own_ref)):
+    for turn, out_ref in zip((2, 1, 0), out_refs):
         first = pl.multiple_of((me ^ turn) * width, width)
         part = partial_sum(cotangent_ref, weight_ref[pl.ds(first, width), :])
         out_ref[...] = part.astype(out_ref.dtype)
@@ -168,29 +164,32 @@
     )
     gathered = (gathered.astype(F32) * (1.0 / scale)).reshape(shares, blocks, rows, width)
     work = tokens * depth * own_width * parts
+    in_hbm = pl.BlockSpec(memory_space=pltpu.HBM)
+    chunk = jax.ShapeDtypeStruct((tokens, own_width), BF16)
     far = kernel_call(
         far_kernel,
-        [jax.ShapeDtypeStruct((tokens, own_width), BF16)] * 2,
-        work,
-        1 << 20,
-        in_specs=[pl.BlockSpec(memory_space=pltpu.VMEM), pl.BlockSpec(memory_space=pltpu.HBM)],
+        chunk,
+        work // 2,
+        1 << 19,
+        in_specs=[in_hbm, in_hbm],
         scratch_shapes=[
-            pltpu.VMEM((2, own_width, depth), BF16),
+            pltpu.VMEM((tokens, depth), BF16),
+            pltpu.VMEM((own_width, depth), BF16),
             pltpu.SemaphoreType.DMA((2,)),
         ],
-    )(cotangent, pltpu.with_memory_space_constraint(base_weight, pltpu.HBM))
-    near, own = kernel_call(
+    )(
+        pltpu.with_memory_space_constraint(cotangent, pltpu.HBM),
+        pltpu.with_memory_space_constraint(base_weight, pltpu.HBM),
+    )
+    side, near, own = kernel_call(
         near_kernel,
-        (
-            jax.ShapeDtypeStruct((tokens, own_width), BF16),
-            jax.ShapeDtypeStruct((tokens, own_width), F32),
-        ),
-        work,
+        (chunk, chunk, jax.ShapeDtypeStruct((tokens, own_width), F32)),
+        work + work // 2,
         1 << 20,
     )(cotangent, base_weight)
     received = [
         lax.ppermute(part, "outcol", [(i, i ^ turn) for i in range(parts)])
-        for turn, part in ((3, far[0]), (2, far[1]), (1, near))
+        for turn, part in ((3, far), (2, side), (1, near))
     ]
     powers = kernel_call(
         powers_kernel,

time: 56.1 us -> 55.9 us (level)
  local copies, waits for them, and re-layouts: 1.58 us -> 0.75 us
  waiting for transfers between devices: 8.14 us -> 8.72 us
    unnamed x6, local copies, waits for them, and re-layouts: 0.85 us -> 0.02 us
  transfers between devices with their start and end apart: 5 -> 5, of which waited for: 2 -> 3; matrix products, arithmetic and copies ran while one was open for 0% -> 0% of each run, Pallas kernels for 10% -> 10%
where the time goes in v7:
time: 55.9 us; the launch traced here: 55.2 us
  starting transfers between devices  35.7 us (64%)
  waiting for transfers between devices  8.72 us (16%)
  Pallas kernels  7.83 us (14%)
  other arithmetic  1.52 us (3%)
  local copies, waits for them, and re-layouts  0.75 us (1%)
  between operations  0.75 us (1%)
    all_to_all x1, starting transfers between devices, body(): lax.all_to_all(jnp.broadcast_to(packed, (shares, blocks * rows, width)),...  16.5 us
    all_to_all x1, starting transfers between devices, body(): lax.all_to_all(sends, 'dp', 0, 0, axis_index_groups=descending, tiled=True)  11.6 us
    ppermute x3, starting transfers between devices, body(): lax.ppermute(part, 'outcol', [(i, i ^ turn) for i in range(parts)])  7.58 us
    all_to_all x1, waiting for transfers between devices, body(): lax.all_to_all(sends, 'dp', 0, 0, axis_index_groups=descending, tiled=True)  6.35 us
    pallas_call x1, Pallas kernels, body(): kernel_call(acts_kernel, jax.ShapeDtypeStruct((tokens, own_width), BF16),...  2.9 us
    pallas_call x1, Pallas kernels, body(): kernel_call(chain_kernel, (jax.ShapeDtypeStruct((tokens, own_width), BF16...  2.32 us
    ppermute x3, waiting for transfers between devices, body(): lax.ppermute(part, 'outcol', [(i, i ^ turn) for i in range(parts)])  1.99 us
    pallas_call x1, Pallas kernels, body(): kernel_call(far_kernel, chunk, work // 2, 1 << 19, in_specs=[in_hbm, in_h...  1.23 us
  transfers between devices with their start and end apart: 5, of which 3 were waited for; matrix products, arithmetic and copies ran while one was open for 0% of the time, Pallas kernels for 10%

profile of v7, /device:TPU:6, one launch (start us, length us, event | category | flops | bytes accessed | tf_op | source)
XLA Modules:
  0.0 55.2 jit_solution(12185267068276300969)
XLA Ops:
  0.6 0.0 copy-start
  0.6 0.8 %fusion = f16[16,256]{1,0:T(8,128)(2,1)S(1)} fusion(f32[2,8,256]{2,1,0:T(8,128)} %param.7), kind=kLoop, calls=%fused_computation.3 | loop fusion | flops 8192 | bytes 24576 | tf_op jit(solution)/shard_map/broadcast_in_dim | solution.py:158
  1.5 0.7 %broadcast_in_dim.8 = f16[32,16,256]{2,1,0:T(8,128)(2,1)} broadcast(f16[16,256]{1,0:T(8,128)(2,1)S(1)} %fusion), dimensions={1,2} | broadcast | bytes 270336 | tf_op jit(solution)/shard_map/broadcast_in_dim | solution.py:158
  2.2 16.5 %all-to-all-start = ((f16[32,16,256]{2,1,0:T(8,128)(2,1)}), f16[32,16,256]{2,1,0:T(8,128)(2,1)S(1)}, u32[]{:S(2)}, u32[]{:S(2)}) async-start(f16[32,16,256]{2,1,0:T(8,128)(2,1)} %broadcast_in_dim.8), calls=%async_computation | async-start | bytes 524288 | tf_op jit(solution)/shard_map/all_to_all | solution.py:157
  18.7 0.0 copy-start.1
  18.7 1.2 %shard_map.61 = bf16[128,512]{1,0:T(8,128)(2,1)S(1)} custom-call(bf16[128,256]{1,0:T(8,128)(2,1)} %cotangent_ref.3, bf16[2048,256]{1,0:T(8,128)(2,1)} %weight_ref.3), custom_call_target="tpu_custom_call" | custom-call | flops 33554432 | bytes 524288 | tf_op jit(solution)/shard_map/pallas_call | solution.py:169
  19.9 2.1 %collective-permute-start = (bf16[128,512]{1,0:T(8,128)(2,1)S(1)}, bf16[128,512]{1,0:T(8,128)(2,1)S(1)}, u32[]{:S(2)}, u32[]{:S(2)}) collective-permute-start(bf16[128,512]{1,0:T(8,128)(2,1)S(1)} %shard_map.61), channel_id=1, source_target_pairs={{0,3},{1,2},{2,1},{3,0},{4,7},{5,6},{6,5},{7,4},{8,11},{9,10},{10,... | collective-permute-start | bytes 393224 | tf_op jit(solution)/shard_map/ppermute | solution.py:191
  22.0 0.0 copy-done
  22.0 0.0 copy-done.1
  22.0 0.4 shard_map.60
  22.4 3.0 %collective-permute-start.1 = (bf16[128,512]{1,0:T(8,128)(2,1)S(1)}, bf16[128,512]{1,0:T(8,128)(2,1)S(1)}, u32[]{:S(2)}, u32[]{:S(2)}) collective-permute-start(bf16[128,512]{1,0:T(8,128)(2,1)S(1)} %get-tuple-element.24), channel_id=1, source_target_pairs={{0,2},{1,3},{2,0},{3,1},{4,6},{5,7},{6,4},{7,5},{8,10},{9,11},{10,... | collective-permute-start | bytes 393224 | tf_op jit(solution)/shard_map/ppermute | solution.py:191
  25.5 2.5 %collective-permute-start.2 = (bf16[128,512]{1,0:T(8,128)(2,1)S(1)}, bf16[128,512]{1,0:T(8,128)(2,1)S(1)}, u32[]{:S(2)}, u32[]{:S(2)}) collective-permute-start(bf16[128,512]{1,0:T(8,128)(2,1)S(1)} %get-tuple-element.25), channel_id=1, source_target_pairs={{0,1},{1,0},{2,3},{3,2},{4,5},{5,4},{6,7},{7,6},{8,9},{9,8},{10,11... | collective-permute-start | bytes 393224 | tf_op jit(solution)/shard_map/ppermute | solution.py:191
  27.9 0.4 all-to-all-done
  28.3 0.1 multiply_bitcast_fusion.gathered_ref
  28.4 0.0 copy-start.2
  28.4 1.0 %shard_map.59 = (bf16[2,256,256]{2,1,0:T(8,128)(2,1)S(1)}, bf16[2,256,256]{2,1,0:T(8,128)(2,1)S(1)}, bf16[2,256,256]{2,1,0:T(8,128)(2,1)S(1)}, bf16[2,256,256]{2...) custom-call(f32[32,2,8,256]{3,2,1,0:T(8,128)S(1)} %multiply_bitcast_, ...), custom_call_target="tpu_custom_call" | custom-call | flops 402653184 | bytes 2097152 | tf_op jit(solution)/shard_map/pallas_call | solution.py:194
  29.4 0.0 collective-permute-done.refs_10_
  29.4 2.0 %collective-permute-done.1.refs_11_ = bf16[128,512]{1,0:T(8,128)(2,1)S(1)} collective-permute-done((bf16[128,512]{1,0:T(8,128)(2,1)S(1)}, bf16[128,512]{1,0:T(8,128)(2,1)S(1)}, u32[]{:S(2)}, u32[]{:S(2)}) %collective-permute-start.1) | collective-permute-done | bytes 131104 | tf_op jit(solution)/shard_map/ppermute | solution.py:191
  31.4 0.0 collective-permute-done.2.refs_12_
  31.4 0.0 copy-done.2
  31.4 2.3 %shard_map.62 = (bf16[128,512]{1,0:T(8,128)(2,1)S(1)}, bf16[32,16,256]{2,1,0:T(8,128)(2,1)}) custom-call(bf16[2,256,256]{2,1,0:T(8,128)(2,1)S(1)} %get-tuple-element.15.refs_0_, bf16[2,256,256]{2,1,0:T(8,128)(2,1)S(1)} %get-tuple-element.16.refs_1_, bf16[2,256,256]{2,1,0:T(8,128)(2,1)S(1)} %get-tuple-element.17.refs_2_, ...), custom_call_target="tpu_custom_call" | custom-call | flops 805306368 | bytes 2097152 | tf_op jit(solution)/shard_map/pallas_call | solution.py:200
  33.7 11.6 %all-to-all-start.1 = ((bf16[32,16,256]{2,1,0:T(8,128)(2,1)}), bf16[32,16,256]{2,1,0:T(8,128)(2,1)S(1)}, u32[]{:S(2)}, u32[]{:S(2)}) async-start(bf16[32,16,256]{2,1,0:T(8,128)(2,1)} %get-tuple-element.27), calls=%async_computation.1 | async-start | bytes 524288 | tf_op jit(solution)/shard_map/all_to_all | solution.py:209
  45.3 2.9 %shard_map.63 = bf16[128,512]{1,0:T(8,128)(2,1)} custom-call(f32[32,2,8,256]{3,2,1,0:T(8,128)S(1)} %multiply_bitcast_fusion.gathered_ref, bf16[128,512]{1,0:T(8,128)(2,1)S(1)} %get-tuple-element.26.features_ref), custom_call_target="tpu_custom_call" | custom-call | flops 671088640 | bytes 1048576 | tf_op jit(solution)/shard_map/pallas_call | solution.py:210
  48.2 6.3 %all-to-all-done.1 = bf16[32,16,256]{2,1,0:T(8,128)(2,1)S(1)} async-done(((bf16[32,16,256]{2,1,0:T(8,128)(2,1)}), bf16[32,16,256]{2,1,0:T(8,128)(2,1)S(1)}, u32[]{:S(2)}, u32[]{:S(2)}) %all-to-all-start.1) | async-done | bytes 262176 | tf_op jit(solution)/shard_map/all_to_all | solution.py:209
  54.6 0.7 %convert_reduce_fusion = f32[16,256]{1,0:T(8,128)} fusion(bf16[32,16,256]{2,1,0:T(8,128)(2,1)S(1)} %all-to-all-done.1), kind=kLoop, calls=%fused_computation | loop fusion | flops 258048 | bytes 278528 | tf_op jit(solution)/shard_map/reduce_sum | solution.py:216
Async XLA Ops:
  0.6 21.4 %copy-start = (bf16[2048,256]{1,0:T(8,128)(2,1)S(1)}, bf16[2048,256]{1,0:T(8,128)(2,1)}, u32[]{:S(2)}) copy-start(bf16[2048,256]{1,0:T(8,128)(2,1)} %weight_ref.3) | copy-start | bytes 3145732
  2.2 26.1 %all-to-all-start = ((f16[32,16,256]{2,1,0:T(8,128)(2,1)}), f16[32,16,256]{2,1,0:T(8,128)(2,1)S(1)}, u32[]{:S(2)}, u32[]{:S(2)}) async-start(f16[32,16,256]{2,1,0:T(8,128)(2,1)} %broadcast_in_dim.8), calls=%async_computation | async-start | bytes 524288 | tf_op jit(solution)/shard_map/all_to_all | solution.py:157
  18.7 3.3 %copy-start.1 = (bf16[128,256]{1,0:T(8,128)(2,1)S(1)}, bf16[128,256]{1,0:T(8,128)(2,1)}, u32[]{:S(2)}) copy-start(bf16[128,256]{1,0:T(8,128)(2,1)} %cotangent_ref.3) | copy-start | bytes 196612
  19.9 9.5 %collective-permute-start = (bf16[128,512]{1,0:T(8,128)(2,1)S(1)}, bf16[128,512]{1,0:T(8,128)(2,1)S(1)}, u32[]{:S(2)}, u32[]{:S(2)}) collective-permute-start(bf16[128,512]{1,0:T(8,128)(2,1)S(1)} %shard_map.61), channel_id=1, source_target_pairs={{0,3},{1,2},{2,1},{3,0},{4,7},{5,6},{6,5},{7,4},{8,11},{9,10},{10,... | collective-permute-start | bytes 393224 | tf_op jit(solution)/shard_map/ppermute | solution.py:191
  22.4 9.0 %collective-permute-start.1 = (bf16[128,512]{1,0:T(8,128)(2,1)S(1)}, bf16[128,512]{1,0:T(8,128)(2,1)S(1)}, u32[]{:S(2)}, u32[]{:S(2)}) collective-permute-start(bf16[128,512]{1,0:T(8,128)(2,1)S(1)} %get-tuple-element.24), channel_id=1, source_target_pairs={{0,2},{1,3},{2,0},{3,1},{4,6},{5,7},{6,4},{7,5},{8,10},{9,11},{10,... | collective-permute-start | bytes 393224 | tf_op jit(solution)/shard_map/ppermute | solution.py:191
  25.5 5.9 %collective-permute-start.2 = (bf16[128,512]{1,0:T(8,128)(2,1)S(1)}, bf16[128,512]{1,0:T(8,128)(2,1)S(1)}, u32[]{:S(2)}, u32[]{:S(2)}) collective-permute-start(bf16[128,512]{1,0:T(8,128)(2,1)S(1)} %get-tuple-element.25), channel_id=1, source_target_pairs={{0,1},{1,0},{2,3},{3,2},{4,5},{5,4},{6,7},{7,6},{8,9},{9,8},{10,11... | collective-permute-start | bytes 393224 | tf_op jit(solution)/shard_map/ppermute | solution.py:191
  28.4 3.0 %copy-start.2 = (bf16[128,512]{1,0:T(8,128)(2,1)S(1)}, bf16[128,512]{1,0:T(8,128)(2,1)}, u32[]{:S(2)}) copy-start(bf16[128,512]{1,0:T(8,128)(2,1)} %refs_8_.1) | copy-start | bytes 393220
  33.7 20.9 %all-to-all-start.1 = ((bf16[32,16,256]{2,1,0:T(8,128)(2,1)}), bf16[32,16,256]{2,1,0:T(8,128)(2,1)S(1)}, u32[]{:S(2)}, u32[]{:S(2)}) async-start(bf16[32,16,256]{2,1,0:T(8,128)(2,1)} %get-tuple-element.27), calls=%async_computation.1 | async-start | bytes 524288 | tf_op jit(solution)/shard_map/all_to_all | solution.py:209

commit v8 on v7

--- a/solution.py
+++ b/solution.py
@@ -17,6 +17,11 @@
 def product(left, right):
     dot = lambda a, b: jnp.dot(a, b, preferred_element_type=F32)
     return dot(left[0], right[0]) + (dot(left[0], right[1]) + dot(left[1], right[0]))
+
+
+def last_order(shares):
+    rows = [list(range(first, first + 8)) for first in range(0, shares, 8)]
+    return [share for row in rows[::-1] for share in row[3::-1] + row[:3:-1]]
 
 
 def factors(gathered, block):
@@ -117,7 +122,7 @@
     pieces = [(total[b] - total[b].T).reshape(shares, -1, width) for b in every]
     sends = jnp.concatenate(pieces, axis=1).astype(BF16)
     for place in range(shares):
-        out_ref[place] = sends[shares - 1 - place]
+        out_ref[place] = sends[last_order(shares)[place]]
 
 
 def acts_kernel(gathered_ref, features_ref, out_ref):
@@ -206,7 +211,7 @@
         2 * 12 * blocks * width**3,
         2 << 20,
     )(*powers, activations, own, *received)
-    arrived = lax.all_to_all(sends, "dp", 0, 0, axis_index_groups=descending, tiled=True)
+    arrived = lax.all_to_all(sends, "dp", 0, 0, axis_index_groups=[last_order(shares)], tiled=True)
     grad_acts = kernel_call(
         acts_kernel,
         jax.ShapeDtypeStruct((tokens, own_width), BF16),

time: 55.9 us -> 54.1 us (0.968)
  the two profiles are of different devices: /device:TPU:6 before, /device:TPU:12 now
where the time goes in v8:
time: 54.1 us; the launch traced here: 53.7 us
  starting transfers between devices  34 us (63%)
  waiting for transfers between devices  8.8 us (16%)
  Pallas kernels  7.82 us (14%)
  other arithmetic  1.52 us (3%)
  local copies, waits for them, and re-layouts  0.75 us (1%)
  between operations  0.75 us (1%)
    all_to_all x1, starting transfers between devices, body(): lax.all_to_all(jnp.broadcast_to(packed, (shares, blocks * rows, width)),...  16.2 us
    all_to_all x1, starting transfers between devices, body(): lax.all_to_all(sends, 'dp', 0, 0, axis_index_groups=[last_order(shares)],...  10.3 us
    ppermute x3, starting transfers between devices, body(): lax.ppermute(part, 'outcol', [(i, i ^ turn) for i in range(parts)])  7.59 us
    all_to_all x1, waiting for transfers between devices, body(): lax.all_to_all(sends, 'dp', 0, 0, axis_index_groups=[last_order(shares)],...  7.22 us
    pallas_call x1, Pallas kernels, body(): kernel_call(acts_kernel, jax.ShapeDtypeStruct((tokens, own_width), BF16),...  2.9 us
    pallas_call x1, Pallas kernels, body(): kernel_call(chain_kernel, (jax.ShapeDtypeStruct((tokens, own_width), BF16...  2.31 us
    pallas_call x1, Pallas kernels, body(): kernel_call(far_kernel, chunk, work // 2, 1 << 19, in_specs=[in_hbm, in_h...  1.23 us
    ppermute x3, waiting for transfers between devices, body(): lax.ppermute(part, 'outcol', [(i, i ^ turn) for i in range(parts)])  1.18 us
  transfers between devices with their start and end apart: 5, of which 3 were waited for; matrix products, arithmetic and copies ran while one was open for 0% of the time, Pallas kernels for 10%

profile of v8, /device:TPU:12, one launch (start us, length us, event | category | flops | bytes accessed | tf_op | source)
XLA Modules:
  0.0 53.7 jit_solution(4778317322285881530)
XLA Ops:
  0.6 0.0 copy-start
  0.6 0.8 %fusion = f16[16,256]{1,0:T(8,128)(2,1)S(1)} fusion(f32[2,8,256]{2,1,0:T(8,128)} %param.7), kind=kLoop, calls=%fused_computation.3 | loop fusion | flops 8192 | bytes 24576 | tf_op jit(solution)/shard_map/broadcast_in_dim | solution.py:163
  1.5 0.7 %broadcast_in_dim.8 = f16[32,16,256]{2,1,0:T(8,128)(2,1)} broadcast(f16[16,256]{1,0:T(8,128)(2,1)S(1)} %fusion), dimensions={1,2} | broadcast | bytes 270336 | tf_op jit(solution)/shard_map/broadcast_in_dim | solution.py:163
  2.2 16.2 %all-to-all-start = ((f16[32,16,256]{2,1,0:T(8,128)(2,1)}), f16[32,16,256]{2,1,0:T(8,128)(2,1)S(1)}, u32[]{:S(2)}, u32[]{:S(2)}) async-start(f16[32,16,256]{2,1,0:T(8,128)(2,1)} %broadcast_in_dim.8), calls=%async_computation | async-start | bytes 524288 | tf_op jit(solution)/shard_map/all_to_all | solution.py:162
  18.4 0.0 copy-start.1
  18.4 1.2 %shard_map.61 = bf16[128,512]{1,0:T(8,128)(2,1)S(1)} custom-call(bf16[128,256]{1,0:T(8,128)(2,1)} %cotangent_ref.3, bf16[2048,256]{1,0:T(8,128)(2,1)} %weight_ref.3), custom_call_target="tpu_custom_call" | custom-call | flops 33554432 | bytes 524288 | tf_op jit(solution)/shard_map/pallas_call | solution.py:174
  19.6 1.9 %collective-permute-start = (bf16[128,512]{1,0:T(8,128)(2,1)S(1)}, bf16[128,512]{1,0:T(8,128)(2,1)S(1)}, u32[]{:S(2)}, u32[]{:S(2)}) collective-permute-start(bf16[128,512]{1,0:T(8,128)(2,1)S(1)} %shard_map.61), channel_id=1, source_target_pairs={{0,3},{1,2},{2,1},{3,0},{4,7},{5,6},{6,5},{7,4},{8,11},{9,10},{10,... | collective-permute-start | bytes 393224 | tf_op jit(solution)/shard_map/ppermute | solution.py:196
  21.5 0.0 copy-done
  21.5 0.0 copy-done.1
  21.6 0.4 shard_map.60
  22.0 2.8 %collective-permute-start.1 = (bf16[128,512]{1,0:T(8,128)(2,1)S(1)}, bf16[128,512]{1,0:T(8,128)(2,1)S(1)}, u32[]{:S(2)}, u32[]{:S(2)}) collective-permute-start(bf16[128,512]{1,0:T(8,128)(2,1)S(1)} %get-tuple-element.24), channel_id=1, source_target_pairs={{0,2},{1,3},{2,0},{3,1},{4,6},{5,7},{6,4},{7,5},{8,10},{9,11},{10,... | collective-permute-start | bytes 393224 | tf_op jit(solution)/shard_map/ppermute | solution.py:196
  24.8 2.9 %collective-permute-start.2 = (bf16[128,512]{1,0:T(8,128)(2,1)S(1)}, bf16[128,512]{1,0:T(8,128)(2,1)S(1)}, u32[]{:S(2)}, u32[]{:S(2)}) collective-permute-start(bf16[128,512]{1,0:T(8,128)(2,1)S(1)} %get-tuple-element.25), channel_id=1, source_target_pairs={{0,1},{1,0},{2,3},{3,2},{4,5},{5,4},{6,7},{7,6},{8,9},{9,8},{10,11... | collective-permute-start | bytes 393224 | tf_op jit(solution)/shard_map/ppermute | solution.py:196
  27.6 0.4 all-to-all-done
  28.0 0.1 multiply_bitcast_fusion.gathered_ref
  28.1 0.0 copy-start.2
  28.1 1.0 %shard_map.59 = (bf16[2,256,256]{2,1,0:T(8,128)(2,1)S(1)}, bf16[2,256,256]{2,1,0:T(8,128)(2,1)S(1)}, bf16[2,256,256]{2,1,0:T(8,128)(2,1)S(1)}, bf16[2,256,256]{2...) custom-call(f32[32,2,8,256]{3,2,1,0:T(8,128)S(1)} %multiply_bitcast_, ...), custom_call_target="tpu_custom_call" | custom-call | flops 402653184 | bytes 2097152 | tf_op jit(solution)/shard_map/pallas_call | solution.py:199
  29.1 0.0 collective-permute-done.refs_10_
  29.1 1.2 %collective-permute-done.1.refs_11_ = bf16[128,512]{1,0:T(8,128)(2,1)S(1)} collective-permute-done((bf16[128,512]{1,0:T(8,128)(2,1)S(1)}, bf16[128,512]{1,0:T(8,128)(2,1)S(1)}, u32[]{:S(2)}, u32[]{:S(2)}) %collective-permute-start.1) | collective-permute-done | bytes 131104 | tf_op jit(solution)/shard_map/ppermute | solution.py:196
  30.3 0.0 collective-permute-done.2.refs_12_
  30.3 0.0 copy-done.2
  30.3 2.3 %shard_map.62 = (bf16[128,512]{1,0:T(8,128)(2,1)S(1)}, bf16[32,16,256]{2,1,0:T(8,128)(2,1)}) custom-call(bf16[2,256,256]{2,1,0:T(8,128)(2,1)S(1)} %get-tuple-element.15.refs_0_, bf16[2,256,256]{2,1,0:T(8,128)(2,1)S(1)} %get-tuple-element.16.refs_1_, bf16[2,256,256]{2,1,0:T(8,128)(2,1)S(1)} %get-tuple-element.17.refs_2_, ...), custom_call_target="tpu_custom_call" | custom-call | flops 805306368 | bytes 2097152 | tf_op jit(solution)/shard_map/pallas_call | solution.py:205
  32.6 10.3 %all-to-all-start.1 = ((bf16[32,16,256]{2,1,0:T(8,128)(2,1)}), bf16[32,16,256]{2,1,0:T(8,128)(2,1)S(1)}, u32[]{:S(2)}, u32[]{:S(2)}) async-start(bf16[32,16,256]{2,1,0:T(8,128)(2,1)} %get-tuple-element.27), calls=%async_computation.1 | async-start | bytes 524288 | tf_op jit(solution)/shard_map/all_to_all | solution.py:214
  42.9 2.9 %shard_map.63 = bf16[128,512]{1,0:T(8,128)(2,1)} custom-call(f32[32,2,8,256]{3,2,1,0:T(8,128)S(1)} %multiply_bitcast_fusion.gathered_ref, bf16[128,512]{1,0:T(8,128)(2,1)S(1)} %get-tuple-element.26.features_ref), custom_call_target="tpu_custom_call" | custom-call | flops 671088640 | bytes 1048576 | tf_op jit(solution)/shard_map/pallas_call | solution.py:215
  45.8 7.2 %all-to-all-done.1 = bf16[32,16,256]{2,1,0:T(8,128)(2,1)S(1)} async-done(((bf16[32,16,256]{2,1,0:T(8,128)(2,1)}), bf16[32,16,256]{2,1,0:T(8,128)(2,1)S(1)}, u32[]{:S(2)}, u32[]{:S(2)}) %all-to-all-start.1) | async-done | bytes 262176 | tf_op jit(solution)/shard_map/all_to_all | solution.py:214
  53.0 0.7 %convert_reduce_fusion = f32[16,256]{1,0:T(8,128)} fusion(bf16[32,16,256]{2,1,0:T(8,128)(2,1)S(1)} %all-to-all-done.1), kind=kLoop, calls=%fused_computation | loop fusion | flops 258048 | bytes 278528 | tf_op jit(solution)/shard_map/reduce_sum | solution.py:221
Async XLA Ops:
  0.6 20.9 %copy-start = (bf16[2048,256]{1,0:T(8,128)(2,1)S(1)}, bf16[2048,256]{1,0:T(8,128)(2,1)}, u32[]{:S(2)}) copy-start(bf16[2048,256]{1,0:T(8,128)(2,1)} %weight_ref.3) | copy-start | bytes 3145732
  2.2 25.9 %all-to-all-start = ((f16[32,16,256]{2,1,0:T(8,128)(2,1)}), f16[32,16,256]{2,1,0:T(8,128)(2,1)S(1)}, u32[]{:S(2)}, u32[]{:S(2)}) async-start(f16[32,16,256]{2,1,0:T(8,128)(2,1)} %broadcast_in_dim.8), calls=%async_computation | async-start | bytes 524288 | tf_op jit(solution)/shard_map/all_to_all | solution.py:162
  18.4 3.2 %copy-start.1 = (bf16[128,256]{1,0:T(8,128)(2,1)S(1)}, bf16[128,256]{1,0:T(8,128)(2,1)}, u32[]{:S(2)}) copy-start(bf16[128,256]{1,0:T(8,128)(2,1)} %cotangent_ref.3) | copy-start | bytes 196612
  19.6 9.5 %collective-permute-start = (bf16[128,512]{1,0:T(8,128)(2,1)S(1)}, bf16[128,512]{1,0:T(8,128)(2,1)S(1)}, u32[]{:S(2)}, u32[]{:S(2)}) collective-permute-start(bf16[128,512]{1,0:T(8,128)(2,1)S(1)} %shard_map.61), channel_id=1, source_target_pairs={{0,3},{1,2},{2,1},{3,0},{4,7},{5,6},{6,5},{7,4},{8,11},{9,10},{10,... | collective-permute-start | bytes 393224 | tf_op jit(solution)/shard_map/ppermute | solution.py:196
  22.0 8.3 %collective-permute-start.1 = (bf16[128,512]{1,0:T(8,128)(2,1)S(1)}, bf16[128,512]{1,0:T(8,128)(2,1)S(1)}, u32[]{:S(2)}, u32[]{:S(2)}) collective-permute-start(bf16[128,512]{1,0:T(8,128)(2,1)S(1)} %get-tuple-element.24), channel_id=1, source_target_pairs={{0,2},{1,3},{2,0},{3,1},{4,6},{5,7},{6,4},{7,5},{8,10},{9,11},{10,... | collective-permute-start | bytes 393224 | tf_op jit(solution)/shard_map/ppermute | solution.py:196
  24.8 5.5 %collective-permute-start.2 = (bf16[128,512]{1,0:T(8,128)(2,1)S(1)}, bf16[128,512]{1,0:T(8,128)(2,1)S(1)}, u32[]{:S(2)}, u32[]{:S(2)}) collective-permute-start(bf16[128,512]{1,0:T(8,128)(2,1)S(1)} %get-tuple-element.25), channel_id=1, source_target_pairs={{0,1},{1,0},{2,3},{3,2},{4,5},{5,4},{6,7},{7,6},{8,9},{9,8},{10,11... | collective-permute-start | bytes 393224 | tf_op jit(solution)/shard_map/ppermute | solution.py:196
  28.1 2.2 %copy-start.2 = (bf16[128,512]{1,0:T(8,128)(2,1)S(1)}, bf16[128,512]{1,0:T(8,128)(2,1)}, u32[]{:S(2)}) copy-start(bf16[128,512]{1,0:T(8,128)(2,1)} %refs_8_.1) | copy-start | bytes 393220
  32.6 20.4 %all-to-all-start.1 = ((bf16[32,16,256]{2,1,0:T(8,128)(2,1)}), bf16[32,16,256]{2,1,0:T(8,128)(2,1)S(1)}, u32[]{:S(2)}, u32[]{:S(2)}) async-start(bf16[32,16,256]{2,1,0:T(8,128)(2,1)} %get-tuple-element.27), calls=%async_computation.1 | async-start | bytes 524288 | tf_op jit(solution)/shard_map/all_to_all | solution.py:214

commit v9 on v8

--- a/solution.py
+++ b/solution.py
@@ -21,7 +21,8 @@
 
 def last_order(shares):
     rows = [list(range(first, first + 8)) for first in range(0, shares, 8)]
-    return [share for row in rows[::-1] for share in row[3::-1] + row[:3:-1]]
+    rows = rows[0::2][::-1] + rows[1::2][::-1]
+    return [share for row in rows for share in row[3::-1] + row[:3:-1]]
 
 
 def factors(gathered, block):

time: 54.1 us -> 53.8 us (level)
  the two profiles are of different devices: /device:TPU:12 before, /device:TPU:6 now
where the time goes in v9:
time: 53.8 us; the launch traced here: 53.3 us
  starting transfers between devices  34.6 us (64%)
  waiting for transfers between devices  7.85 us (15%)
  Pallas kernels  7.83 us (15%)
  other arithmetic  1.52 us (3%)
  local copies, waits for them, and re-layouts  0.75 us (1%)
  between operations  0.75 us (1%)
    all_to_all x1, starting transfers between devices, body(): lax.all_to_all(jnp.broadcast_to(packed, (shares, blocks * rows, width)),...  16.5 us
    all_to_all x1, starting transfers between devices, body(): lax.all_to_all(sends, 'dp', 0, 0, axis_index_groups=[last_order(shares)],...  10.6 us
    ppermute x3, starting transfers between devices, body(): lax.ppermute(part, 'outcol', [(i, i ^ turn) for i in range(parts)])  7.58 us
    all_to_all x1, waiting for transfers between devices, body(): lax.all_to_all(sends, 'dp', 0, 0, axis_index_groups=[last_order(shares)],...  5.48 us
    pallas_call x1, Pallas kernels, body(): kernel_call(acts_kernel, jax.ShapeDtypeStruct((tokens, own_width), BF16),...  2.9 us
    pallas_call x1, Pallas kernels, body(): kernel_call(chain_kernel, (jax.ShapeDtypeStruct((tokens, own_width), BF16...  2.32 us
    ppermute x3, waiting for transfers between devices, body(): lax.ppermute(part, 'outcol', [(i, i ^ turn) for i in range(parts)])  1.99 us
    pallas_call x1, Pallas kernels, body(): kernel_call(far_kernel, chunk, work // 2, 1 << 19, in_specs=[in_hbm, in_h...  1.23 us
  transfers between devices with their start and end apart: 5, of which 3 were waited for; matrix products, arithmetic and copies ran while one was open for 0% of the time, Pallas kernels for 10%

profile of v9, /device:TPU:6, one launch (start us, length us, event | category | flops | bytes accessed | tf_op | source)
XLA Modules:
  0.0 53.3 jit_solution(5438995403918020035)
XLA Ops:
  0.6 0.0 copy-start
  0.6 0.8 %fusion = f16[16,256]{1,0:T(8,128)(2,1)S(1)} fusion(f32[2,8,256]{2,1,0:T(8,128)} %param.7), kind=kLoop, calls=%fused_computation.3 | loop fusion | flops 8192 | bytes 24576 | tf_op jit(solution)/shard_map/broadcast_in_dim | solution.py:164
  1.5 0.7 %broadcast_in_dim.8 = f16[32,16,256]{2,1,0:T(8,128)(2,1)} broadcast(f16[16,256]{1,0:T(8,128)(2,1)S(1)} %fusion), dimensions={1,2} | broadcast | bytes 270336 | tf_op jit(solution)/shard_map/broadcast_in_dim | solution.py:164
  2.2 16.5 %all-to-all-start = ((f16[32,16,256]{2,1,0:T(8,128)(2,1)}), f16[32,16,256]{2,1,0:T(8,128)(2,1)S(1)}, u32[]{:S(2)}, u32[]{:S(2)}) async-start(f16[32,16,256]{2,1,0:T(8,128)(2,1)} %broadcast_in_dim.8), calls=%async_computation | async-start | bytes 524288 | tf_op jit(solution)/shard_map/all_to_all | solution.py:163
  18.7 0.0 copy-start.1
  18.7 1.2 %shard_map.61 = bf16[128,512]{1,0:T(8,128)(2,1)S(1)} custom-call(bf16[128,256]{1,0:T(8,128)(2,1)} %cotangent_ref.3, bf16[2048,256]{1,0:T(8,128)(2,1)} %weight_ref.3), custom_call_target="tpu_custom_call" | custom-call | flops 33554432 | bytes 524288 | tf_op jit(solution)/shard_map/pallas_call | solution.py:175
  19.9 2.1 %collective-permute-start = (bf16[128,512]{1,0:T(8,128)(2,1)S(1)}, bf16[128,512]{1,0:T(8,128)(2,1)S(1)}, u32[]{:S(2)}, u32[]{:S(2)}) collective-permute-start(bf16[128,512]{1,0:T(8,128)(2,1)S(1)} %shard_map.61), channel_id=1, source_target_pairs={{0,3},{1,2},{2,1},{3,0},{4,7},{5,6},{6,5},{7,4},{8,11},{9,10},{10,... | collective-permute-start | bytes 393224 | tf_op jit(solution)/shard_map/ppermute | solution.py:197
  22.0 0.0 copy-done
  22.0 0.0 copy-done.1
  22.0 0.4 shard_map.60
  22.4 3.0 %collective-permute-start.1 = (bf16[128,512]{1,0:T(8,128)(2,1)S(1)}, bf16[128,512]{1,0:T(8,128)(2,1)S(1)}, u32[]{:S(2)}, u32[]{:S(2)}) collective-permute-start(bf16[128,512]{1,0:T(8,128)(2,1)S(1)} %get-tuple-element.24), channel_id=1, source_target_pairs={{0,2},{1,3},{2,0},{3,1},{4,6},{5,7},{6,4},{7,5},{8,10},{9,11},{10,... | collective-permute-start | bytes 393224 | tf_op jit(solution)/shard_map/ppermute | solution.py:197
  25.5 2.5 %collective-permute-start.2 = (bf16[128,512]{1,0:T(8,128)(2,1)S(1)}, bf16[128,512]{1,0:T(8,128)(2,1)S(1)}, u32[]{:S(2)}, u32[]{:S(2)}) collective-permute-start(bf16[128,512]{1,0:T(8,128)(2,1)S(1)} %get-tuple-element.25), channel_id=1, source_target_pairs={{0,1},{1,0},{2,3},{3,2},{4,5},{5,4},{6,7},{7,6},{8,9},{9,8},{10,11... | collective-permute-start | bytes 393224 | tf_op jit(solution)/shard_map/ppermute | solution.py:197
  27.9 0.4 all-to-all-done
  28.3 0.1 multiply_bitcast_fusion.gathered_ref
  28.4 0.0 copy-start.2
  28.4 1.0 %shard_map.59 = (bf16[2,256,256]{2,1,0:T(8,128)(2,1)S(1)}, bf16[2,256,256]{2,1,0:T(8,128)(2,1)S(1)}, bf16[2,256,256]{2,1,0:T(8,128)(2,1)S(1)}, bf16[2,256,256]{2...) custom-call(f32[32,2,8,256]{3,2,1,0:T(8,128)S(1)} %multiply_bitcast_, ...), custom_call_target="tpu_custom_call" | custom-call | flops 402653184 | bytes 2097152 | tf_op jit(solution)/shard_map/pallas_call | solution.py:200
  29.4 0.0 collective-permute-done.refs_10_
  29.4 2.0 %collective-permute-done.1.refs_11_ = bf16[128,512]{1,0:T(8,128)(2,1)S(1)} collective-permute-done((bf16[128,512]{1,0:T(8,128)(2,1)S(1)}, bf16[128,512]{1,0:T(8,128)(2,1)S(1)}, u32[]{:S(2)}, u32[]{:S(2)}) %collective-permute-start.1) | collective-permute-done | bytes 131104 | tf_op jit(solution)/shard_map/ppermute | solution.py:197
  31.4 0.0 collective-permute-done.2.refs_12_
  31.4 0.0 copy-done.2
  31.4 2.3 %shard_map.62 = (bf16[128,512]{1,0:T(8,128)(2,1)S(1)}, bf16[32,16,256]{2,1,0:T(8,128)(2,1)}) custom-call(bf16[2,256,256]{2,1,0:T(8,128)(2,1)S(1)} %get-tuple-element.15.refs_0_, bf16[2,256,256]{2,1,0:T(8,128)(2,1)S(1)} %get-tuple-element.16.refs_1_, bf16[2,256,256]{2,1,0:T(8,128)(2,1)S(1)} %get-tuple-element.17.refs_2_, ...), custom_call_target="tpu_custom_call" | custom-call | flops 805306368 | bytes 2097152 | tf_op jit(solution)/shard_map/pallas_call | solution.py:206
  33.7 10.6 %all-to-all-start.1 = ((bf16[32,16,256]{2,1,0:T(8,128)(2,1)}), bf16[32,16,256]{2,1,0:T(8,128)(2,1)S(1)}, u32[]{:S(2)}, u32[]{:S(2)}) async-start(bf16[32,16,256]{2,1,0:T(8,128)(2,1)} %get-tuple-element.27), calls=%async_computation.1 | async-start | bytes 524288 | tf_op jit(solution)/shard_map/all_to_all | solution.py:215
  44.3 2.9 %shard_map.63 = bf16[128,512]{1,0:T(8,128)(2,1)} custom-call(f32[32,2,8,256]{3,2,1,0:T(8,128)S(1)} %multiply_bitcast_fusion.gathered_ref, bf16[128,512]{1,0:T(8,128)(2,1)S(1)} %get-tuple-element.26.features_ref), custom_call_target="tpu_custom_call" | custom-call | flops 671088640 | bytes 1048576 | tf_op jit(solution)/shard_map/pallas_call | solution.py:216
  47.2 5.5 %all-to-all-done.1 = bf16[32,16,256]{2,1,0:T(8,128)(2,1)S(1)} async-done(((bf16[32,16,256]{2,1,0:T(8,128)(2,1)}), bf16[32,16,256]{2,1,0:T(8,128)(2,1)S(1)}, u32[]{:S(2)}, u32[]{:S(2)}) %all-to-all-start.1) | async-done | bytes 262176 | tf_op jit(solution)/shard_map/all_to_all | solution.py:215
  52.7 0.7 %convert_reduce_fusion = f32[16,256]{1,0:T(8,128)} fusion(bf16[32,16,256]{2,1,0:T(8,128)(2,1)S(1)} %all-to-all-done.1), kind=kLoop, calls=%fused_computation | loop fusion | flops 258048 | bytes 278528 | tf_op jit(solution)/shard_map/reduce_sum | solution.py:222
Async XLA Ops:
  0.6 21.4 %copy-start = (bf16[2048,256]{1,0:T(8,128)(2,1)S(1)}, bf16[2048,256]{1,0:T(8,128)(2,1)}, u32[]{:S(2)}) copy-start(bf16[2048,256]{1,0:T(8,128)(2,1)} %weight_ref.3) | copy-start | bytes 3145732
  2.2 26.1 %all-to-all-start = ((f16[32,16,256]{2,1,0:T(8,128)(2,1)}), f16[32,16,256]{2,1,0:T(8,128)(2,1)S(1)}, u32[]{:S(2)}, u32[]{:S(2)}) async-start(f16[32,16,256]{2,1,0:T(8,128)(2,1)} %broadcast_in_dim.8), calls=%async_computation | async-start | bytes 524288 | tf_op jit(solution)/shard_map/all_to_all | solution.py:163
  18.7 3.3 %copy-start.1 = (bf16[128,256]{1,0:T(8,128)(2,1)S(1)}, bf16[128,256]{1,0:T(8,128)(2,1)}, u32[]{:S(2)}) copy-start(bf16[128,256]{1,0:T(8,128)(2,1)} %cotangent_ref.3) | copy-start | bytes 196612
  19.9 9.5 %collective-permute-start = (bf16[128,512]{1,0:T(8,128)(2,1)S(1)}, bf16[128,512]{1,0:T(8,128)(2,1)S(1)}, u32[]{:S(2)}, u32[]{:S(2)}) collective-permute-start(bf16[128,512]{1,0:T(8,128)(2,1)S(1)} %shard_map.61), channel_id=1, source_target_pairs={{0,3},{1,2},{2,1},{3,0},{4,7},{5,6},{6,5},{7,4},{8,11},{9,10},{10,... | collective-permute-start | bytes 393224 | tf_op jit(solution)/shard_map/ppermute | solution.py:197
  22.4 9.0 %collective-permute-start.1 = (bf16[128,512]{1,0:T(8,128)(2,1)S(1)}, bf16[128,512]{1,0:T(8,128)(2,1)S(1)}, u32[]{:S(2)}, u32[]{:S(2)}) collective-permute-start(bf16[128,512]{1,0:T(8,128)(2,1)S(1)} %get-tuple-element.24), channel_id=1, source_target_pairs={{0,2},{1,3},{2,0},{3,1},{4,6},{5,7},{6,4},{7,5},{8,10},{9,11},{10,... | collective-permute-start | bytes 393224 | tf_op jit(solution)/shard_map/ppermute | solution.py:197
  25.5 5.9 %collective-permute-start.2 = (bf16[128,512]{1,0:T(8,128)(2,1)S(1)}, bf16[128,512]{1,0:T(8,128)(2,1)S(1)}, u32[]{:S(2)}, u32[]{:S(2)}) collective-permute-start(bf16[128,512]{1,0:T(8,128)(2,1)S(1)} %get-tuple-element.25), channel_id=1, source_target_pairs={{0,1},{1,0},{2,3},{3,2},{4,5},{5,4},{6,7},{7,6},{8,9},{9,8},{10,11... | collective-permute-start | bytes 393224 | tf_op jit(solution)/shard_map/ppermute | solution.py:197
  28.4 3.0 %copy-start.2 = (bf16[128,512]{1,0:T(8,128)(2,1)S(1)}, bf16[128,512]{1,0:T(8,128)(2,1)}, u32[]{:S(2)}) copy-start(bf16[128,512]{1,0:T(8,128)(2,1)} %refs_8_.1) | copy-start | bytes 393220
  33.7 19.0 %all-to-all-start.1 = ((bf16[32,16,256]{2,1,0:T(8,128)(2,1)}), bf16[32,16,256]{2,1,0:T(8,128)(2,1)S(1)}, u32[]{:S(2)}, u32[]{:S(2)}) async-start(bf16[32,16,256]{2,1,0:T(8,128)(2,1)} %get-tuple-element.27), calls=%async_computation.1 | async-start | bytes 524288 | tf_op jit(solution)/shard_map/all_to_all | solution.py:215

commit v10 on v8

--- a/solution.py
+++ b/solution.py
@@ -19,15 +19,18 @@
     return dot(left[0], right[0]) + (dot(left[0], right[1]) + dot(left[1], right[0]))
 
 
+def first_order(shares):
+    return [8*y+z for y in (1, 0, 3, 2) for z in (7, 6, 5, 4, 3, 2, 1, 0)]
+
+
 def last_order(shares):
-    rows = [list(range(first, first + 8)) for first in range(0, shares, 8)]
-    return [share for row in rows[::-1] for share in row[3::-1] + row[:3:-1]]
+    return [8*y+z for y in (2, 0, 3, 1) for z in (3, 7, 2, 6, 1, 5, 0, 4)]
 
 
 def factors(gathered, block):
     shares = gathered.shape[0]
     param = jnp.concatenate(
-        [gathered[shares - 1 - share, block] for share in range(shares)], axis=0
+        [gathered[first_order(shares).index(share), block] for share in range(shares)], axis=0
     )
     skew = param - param.T
     skew_pair = split(skew)
@@ -70,7 +73,7 @@
     shares, blocks, rows, width = gathered_ref.shape
     every = range(blocks)
     param = [
-        jnp.concatenate([gathered_ref[shares - 1 - share, b] for share in range(shares)], axis=0)
+        jnp.concatenate([gathered_ref[first_order(shares).index(share), b] for share in range(shares)], axis=0)
         for b in every
     ]
     skew = [param[b] - param[b].T for b in every]
@@ -158,13 +161,12 @@
     blocks, rows, width = skew_param.shape
     scale = 65536.0
     packed = (skew_param * scale).astype(jnp.float16).reshape(1, blocks * rows, width)
-    descending = [list(range(shares - 1, -1, -1))]
     gathered = lax.all_to_all(
         jnp.broadcast_to(packed, (shares, blocks * rows, width)),
         "dp",
         0,
         0,
-        axis_index_groups=descending,
+        axis_index_groups=[first_order(shares)],
         tiled=True,
     )
     gathered = (gathered.astype(F32) * (1.0 / scale)).reshape(shares, blocks, rows, width)

time: 54.1 us -> 54.1 us (level)
  the two profiles are of different devices: /device:TPU:12 before, /device:TPU:6 now
where the time goes in v10:
time: 54.1 us; the launch traced here: 53.2 us
  starting transfers between devices  35.9 us (66%)
  Pallas kernels  7.82 us (14%)
  waiting for transfers between devices  6.44 us (12%)
  other arithmetic  1.52 us (3%)
  local copies, waits for them, and re-layouts  0.75 us (1%)
  between operations  0.75 us (1%)
    all_to_all x1, starting transfers between devices, body(): lax.all_to_all(jnp.broadcast_to(packed, (shares, blocks * rows, width)),...  16.5 us
    all_to_all x1, starting transfers between devices, body(): lax.all_to_all(sends, 'dp', 0, 0, axis_index_groups=[last_order(shares)],...  11.8 us
    ppermute x3, starting transfers between devices, body(): lax.ppermute(part, 'outcol', [(i, i ^ turn) for i in range(parts)])  7.59 us
    all_to_all x1, waiting for transfers between devices, body(): lax.all_to_all(sends, 'dp', 0, 0, axis_index_groups=[last_order(shares)],...  4.78 us
    pallas_call x1, Pallas kernels, body(): kernel_call(acts_kernel, jax.ShapeDtypeStruct((tokens, own_width), BF16),...  2.9 us
    pallas_call x1, Pallas kernels, body(): kernel_call(chain_kernel, (jax.ShapeDtypeStruct((tokens, own_width), BF16...  2.31 us
    all_to_all x1, waiting for transfers between devices, body(): lax.all_to_all(jnp.broadcast_to(packed, (shares, blocks * rows, width)),...  1.34 us
    pallas_call x1, Pallas kernels, body(): kernel_call(far_kernel, chunk, work // 2, 1 << 19, in_specs=[in_hbm, in_h...  1.23 us
  transfers between devices with their start and end apart: 5, of which 3 were waited for; matrix products, arithmetic and copies ran while one was open for 0% of the time, Pallas kernels for 10%

profile of v10, /device:TPU:6, one launch (start us, length us, event | category | flops | bytes accessed | tf_op | source)
XLA Modules:
  0.0 53.2 jit_solution(11859283981035309388)
XLA Ops:
  0.6 0.0 copy-start
  0.6 0.8 %fusion = f16[16,256]{1,0:T(8,128)(2,1)S(1)} fusion(f32[2,8,256]{2,1,0:T(8,128)} %param.7), kind=kLoop, calls=%fused_computation.3 | loop fusion | flops 8192 | bytes 24576 | tf_op jit(solution)/shard_map/broadcast_in_dim | solution.py:165
  1.5 0.7 %broadcast_in_dim.8 = f16[32,16,256]{2,1,0:T(8,128)(2,1)} broadcast(f16[16,256]{1,0:T(8,128)(2,1)S(1)} %fusion), dimensions={1,2} | broadcast | bytes 270336 | tf_op jit(solution)/shard_map/broadcast_in_dim | solution.py:165
  2.2 16.5 %all-to-all-start = ((f16[32,16,256]{2,1,0:T(8,128)(2,1)}), f16[32,16,256]{2,1,0:T(8,128)(2,1)S(1)}, u32[]{:S(2)}, u32[]{:S(2)}) async-start(f16[32,16,256]{2,1,0:T(8,128)(2,1)} %broadcast_in_dim.8), calls=%async_computation | async-start | bytes 524288 | tf_op jit(solution)/shard_map/all_to_all | solution.py:164
  18.7 0.0 copy-start.1
  18.7 1.2 %shard_map.61 = bf16[128,512]{1,0:T(8,128)(2,1)S(1)} custom-call(bf16[128,256]{1,0:T(8,128)(2,1)} %cotangent_ref.3, bf16[2048,256]{1,0:T(8,128)(2,1)} %weight_ref.3), custom_call_target="tpu_custom_call" | custom-call | flops 33554432 | bytes 524288 | tf_op jit(solution)/shard_map/pallas_call | solution.py:176
  20.0 1.9 %collective-permute-start = (bf16[128,512]{1,0:T(8,128)(2,1)S(1)}, bf16[128,512]{1,0:T(8,128)(2,1)S(1)}, u32[]{:S(2)}, u32[]{:S(2)}) collective-permute-start(bf16[128,512]{1,0:T(8,128)(2,1)S(1)} %shard_map.61), channel_id=1, source_target_pairs={{0,3},{1,2},{2,1},{3,0},{4,7},{5,6},{6,5},{7,4},{8,11},{9,10},{10,... | collective-permute-start | bytes 393224 | tf_op jit(solution)/shard_map/ppermute | solution.py:198
  21.9 0.0 copy-done
  21.9 0.0 copy-done.1
  21.9 0.4 shard_map.60
  22.3 2.8 %collective-permute-start.1 = (bf16[128,512]{1,0:T(8,128)(2,1)S(1)}, bf16[128,512]{1,0:T(8,128)(2,1)S(1)}, u32[]{:S(2)}, u32[]{:S(2)}) collective-permute-start(bf16[128,512]{1,0:T(8,128)(2,1)S(1)} %get-tuple-element.24), channel_id=1, source_target_pairs={{0,2},{1,3},{2,0},{3,1},{4,6},{5,7},{6,4},{7,5},{8,10},{9,11},{10,... | collective-permute-start | bytes 393224 | tf_op jit(solution)/shard_map/ppermute | solution.py:198
  25.1 2.9 %collective-permute-start.2 = (bf16[128,512]{1,0:T(8,128)(2,1)S(1)}, bf16[128,512]{1,0:T(8,128)(2,1)S(1)}, u32[]{:S(2)}, u32[]{:S(2)}) collective-permute-start(bf16[128,512]{1,0:T(8,128)(2,1)S(1)} %get-tuple-element.25), channel_id=1, source_target_pairs={{0,1},{1,0},{2,3},{3,2},{4,5},{5,4},{6,7},{7,6},{8,9},{9,8},{10,11... | collective-permute-start | bytes 393224 | tf_op jit(solution)/shard_map/ppermute | solution.py:198
  28.0 1.3 %all-to-all-done = f16[32,16,256]{2,1,0:T(8,128)(2,1)S(1)} async-done(((f16[32,16,256]{2,1,0:T(8,128)(2,1)}), f16[32,16,256]{2,1,0:T(8,128)(2,1)S(1)}, u32[]{:S(2)}, u32[]{:S(2)}) %all-to-all-start) | async-done | bytes 262176 | tf_op jit(solution)/shard_map/all_to_all | solution.py:164
  29.4 0.1 multiply_bitcast_fusion.gathered_ref
  29.4 0.0 copy-start.2
  29.4 1.0 %shard_map.59 = (bf16[2,256,256]{2,1,0:T(8,128)(2,1)S(1)}, bf16[2,256,256]{2,1,0:T(8,128)(2,1)S(1)}, bf16[2,256,256]{2,1,0:T(8,128)(2,1)S(1)}, bf16[2,256,256]{2...) custom-call(f32[32,2,8,256]{3,2,1,0:T(8,128)S(1)} %multiply_bitcast_, ...), custom_call_target="tpu_custom_call" | custom-call | flops 402653184 | bytes 2097152 | tf_op jit(solution)/shard_map/pallas_call | solution.py:201
  30.4 0.0 collective-permute-done.refs_10_
  30.4 0.3 collective-permute-done.1.refs_11_
  30.7 0.0 collective-permute-done.2.refs_12_
  30.7 0.0 copy-done.2
  30.7 2.3 %shard_map.62 = (bf16[128,512]{1,0:T(8,128)(2,1)S(1)}, bf16[32,16,256]{2,1,0:T(8,128)(2,1)}) custom-call(bf16[2,256,256]{2,1,0:T(8,128)(2,1)S(1)} %get-tuple-element.15.refs_0_, bf16[2,256,256]{2,1,0:T(8,128)(2,1)S(1)} %get-tuple-element.16.refs_1_, bf16[2,256,256]{2,1,0:T(8,128)(2,1)S(1)} %get-tuple-element.17.refs_2_, ...), custom_call_target="tpu_custom_call" | custom-call | flops 805306368 | bytes 2097152 | tf_op jit(solution)/shard_map/pallas_call | solution.py:207
  33.1 11.8 %all-to-all-start.1 = ((bf16[32,16,256]{2,1,0:T(8,128)(2,1)}), bf16[32,16,256]{2,1,0:T(8,128)(2,1)S(1)}, u32[]{:S(2)}, u32[]{:S(2)}) async-start(bf16[32,16,256]{2,1,0:T(8,128)(2,1)} %get-tuple-element.27), calls=%async_computation.1 | async-start | bytes 524288 | tf_op jit(solution)/shard_map/all_to_all | solution.py:216
  44.9 2.9 %shard_map.63 = bf16[128,512]{1,0:T(8,128)(2,1)} custom-call(f32[32,2,8,256]{3,2,1,0:T(8,128)S(1)} %multiply_bitcast_fusion.gathered_ref, bf16[128,512]{1,0:T(8,128)(2,1)S(1)} %get-tuple-element.26.features_ref), custom_call_target="tpu_custom_call" | custom-call | flops 671088640 | bytes 1048576 | tf_op jit(solution)/shard_map/pallas_call | solution.py:217
  47.8 4.8 %all-to-all-done.1 = bf16[32,16,256]{2,1,0:T(8,128)(2,1)S(1)} async-done(((bf16[32,16,256]{2,1,0:T(8,128)(2,1)}), bf16[32,16,256]{2,1,0:T(8,128)(2,1)S(1)}, u32[]{:S(2)}, u32[]{:S(2)}) %all-to-all-start.1) | async-done | bytes 262176 | tf_op jit(solution)/shard_map/all_to_all | solution.py:216
  52.6 0.7 %convert_reduce_fusion = f32[16,256]{1,0:T(8,128)} fusion(bf16[32,16,256]{2,1,0:T(8,128)(2,1)S(1)} %all-to-all-done.1), kind=kLoop, calls=%fused_computation | loop fusion | flops 258048 | bytes 278528 | tf_op jit(solution)/shard_map/reduce_sum | solution.py:223
Async XLA Ops:
  0.6 21.3 %copy-start = (bf16[2048,256]{1,0:T(8,128)(2,1)S(1)}, bf16[2048,256]{1,0:T(8,128)(2,1)}, u32[]{:S(2)}) copy-start(bf16[2048,256]{1,0:T(8,128)(2,1)} %weight_ref.3) | copy-start | bytes 3145732
  2.2 27.2 %all-to-all-start = ((f16[32,16,256]{2,1,0:T(8,128)(2,1)}), f16[32,16,256]{2,1,0:T(8,128)(2,1)S(1)}, u32[]{:S(2)}, u32[]{:S(2)}) async-start(f16[32,16,256]{2,1,0:T(8,128)(2,1)} %broadcast_in_dim.8), calls=%async_computation | async-start | bytes 524288 | tf_op jit(solution)/shard_map/all_to_all | solution.py:164
  18.7 3.2 %copy-start.1 = (bf16[128,256]{1,0:T(8,128)(2,1)S(1)}, bf16[128,256]{1,0:T(8,128)(2,1)}, u32[]{:S(2)}) copy-start(bf16[128,256]{1,0:T(8,128)(2,1)} %cotangent_ref.3) | copy-start | bytes 196612
  20.0 10.4 %collective-permute-start = (bf16[128,512]{1,0:T(8,128)(2,1)S(1)}, bf16[128,512]{1,0:T(8,128)(2,1)S(1)}, u32[]{:S(2)}, u32[]{:S(2)}) collective-permute-start(bf16[128,512]{1,0:T(8,128)(2,1)S(1)} %shard_map.61), channel_id=1, source_target_pairs={{0,3},{1,2},{2,1},{3,0},{4,7},{5,6},{6,5},{7,4},{8,11},{9,10},{10,... | collective-permute-start | bytes 393224 | tf_op jit(solution)/shard_map/ppermute | solution.py:198
  22.3 8.4 %collective-permute-start.1 = (bf16[128,512]{1,0:T(8,128)(2,1)S(1)}, bf16[128,512]{1,0:T(8,128)(2,1)S(1)}, u32[]{:S(2)}, u32[]{:S(2)}) collective-permute-start(bf16[128,512]{1,0:T(8,128)(2,1)S(1)} %get-tuple-element.24), channel_id=1, source_target_pairs={{0,2},{1,3},{2,0},{3,1},{4,6},{5,7},{6,4},{7,5},{8,10},{9,11},{10,... | collective-permute-start | bytes 393224 | tf_op jit(solution)/shard_map/ppermute | solution.py:198
  25.1 5.6 %collective-permute-start.2 = (bf16[128,512]{1,0:T(8,128)(2,1)S(1)}, bf16[128,512]{1,0:T(8,128)(2,1)S(1)}, u32[]{:S(2)}, u32[]{:S(2)}) collective-permute-start(bf16[128,512]{1,0:T(8,128)(2,1)S(1)} %get-tuple-element.25), channel_id=1, source_target_pairs={{0,1},{1,0},{2,3},{3,2},{4,5},{5,4},{6,7},{7,6},{8,9},{9,8},{10,11... | collective-permute-start | bytes 393224 | tf_op jit(solution)/shard_map/ppermute | solution.py:198
  29.4 1.3 %copy-start.2 = (bf16[128,512]{1,0:T(8,128)(2,1)S(1)}, bf16[128,512]{1,0:T(8,128)(2,1)}, u32[]{:S(2)}) copy-start(bf16[128,512]{1,0:T(8,128)(2,1)} %refs_8_.1) | copy-start | bytes 393220
  33.1 19.5 %all-to-all-start.1 = ((bf16[32,16,256]{2,1,0:T(8,128)(2,1)}), bf16[32,16,256]{2,1,0:T(8,128)(2,1)S(1)}, u32[]{:S(2)}, u32[]{:S(2)}) async-start(bf16[32,16,256]{2,1,0:T(8,128)(2,1)} %get-tuple-element.27), calls=%async_computation.1 | async-start | bytes 524288 | tf_op jit(solution)/shard_map/all_to_all | solution.py:216
